TPU v7x, 256 devices: a whole 4x4x8 slice. The times are simulated.
256 devices in a mesh: seq: 64 (over z, y, core), grp: 4 (over x).
Axes of the slice: x: 4, y: 4, z: 8, core: 2. Of those that a mesh axis runs over, the one named last changes fastest.
Arguments:
- queries: bfloat16 [4, 8192, 8192], P('grp', 'seq'), may hold values from -48 to 48
- cotangent: bfloat16 [4, 8192, 8192], P('grp', 'seq'), may hold values from -6 to 6
- cache_keys: bfloat16 [32, 128, 8192], P('grp', None, 'seq'), may hold values from -4.5 to 4.5
- cache_values: bfloat16 [32, 128, 8192], P('grp', None, 'seq'), may hold values from -6 to 6
- block_table: int32 [4, 128, 2], P('grp'), may hold values from 0 to 31, as said below
- block_slot: int32 [32], replicated, may hold values from 0 to 31, as said below
Outputs:
- attended: bfloat16 [4, 8192, 8192], P('grp', 'seq')
- grad_queries: bfloat16 [4, 8192, 8192], P('grp', 'seq')
- grad_keys: bfloat16 [32, 128, 8192], P('grp', None, 'seq')
- grad_values: bfloat16 [32, 128, 8192], P('grp', None, 'seq')
Inputs may be any that keep to these rules, and one draw needn't show every extreme that they name: `block_table`: the 2 block ids of one group differ. Every number of 0 to 31 appears once; block id b is held in row block_slot[b] of cache_keys and cache_values.
All inputs are finite; a program needn't handle non-finite values.
Results may differ from a plain program's by a relative error of at most 0.009.
Values may be sent and summed in bfloat16 or wider, within the bound.
A program may use at most 192 MiB of HBM per device.

v0:
```python
import math

import jax
import jax.numpy as jnp
from jax import lax
from jax.sharding import PartitionSpec as P

HEAD_DIM = 128
GROUP = 64
NEIGHBOURS = 2
NEIGH_LEN = 128


def on_device(queries, cotangent, cache_keys, cache_values, block_table, block_slot):
    width_here = cache_keys.shape[2]
    heads_here = width_here // HEAD_DIM
    stored = cache_keys.shape[0]
    score_scale = 1.0 / math.sqrt(HEAD_DIM)
    query_heads, cotan_heads = (
        lax.all_to_all(queries[0], "seq", split_axis=1, concat_axis=0, tiled=True),
        lax.all_to_all(cotangent[0], "seq", split_axis=1, concat_axis=0, tiled=True),
    )
    groups = query_heads.shape[0] // GROUP
    flat_table = block_table[0].reshape(-1)
    matches = flat_table[:, None] == jnp.arange(block_slot.shape[0], dtype=jnp.int32)[None, :]
    cache_rows = jnp.sum(jnp.where(matches, block_slot[None, :], 0), axis=1)
    whole_keys, whole_values = (
        lax.all_gather(cache_keys, "grp", axis=0, tiled=True),
        lax.all_gather(cache_values, "grp", axis=0, tiled=True),
    )
    total_rows = whole_keys.shape[0]
    near_keys = jnp.take(whole_keys, cache_rows, axis=0).reshape(
        groups, NEIGHBOURS * NEIGH_LEN, heads_here, HEAD_DIM
    )
    near_values = jnp.take(whole_values, cache_rows, axis=0).reshape(
        groups, NEIGHBOURS * NEIGH_LEN, heads_here, HEAD_DIM
    )
    query_blocks = query_heads.reshape(groups, GROUP, heads_here, HEAD_DIM)
    scores = (
        jnp.einsum("cqhd,ckhd->chqk", query_blocks, near_keys, preferred_element_type=jnp.float32)
        * score_scale
    )
    row_max = jnp.max(scores, axis=-1, keepdims=True)
    weights = jnp.exp(scores - row_max)
    prob = weights / jnp.sum(weights, axis=-1, keepdims=True)
    prob_low = prob.astype(jnp.bfloat16)
    attended = jnp.einsum(
        "chqk,ckhd->cqhd", prob_low, near_values, preferred_element_type=jnp.float32
    )
    attended = attended.astype(jnp.bfloat16).reshape(-1, width_here)
    cotan_blocks = cotan_heads.reshape(groups, GROUP, heads_here, HEAD_DIM)
    prob_grad = jnp.einsum(
        "cqhd,ckhd->chqk", cotan_blocks, near_values, preferred_element_type=jnp.float32
    )
    row_dot = jnp.sum(prob * prob_grad, axis=-1, keepdims=True)
    score_grad = (score_scale * prob * (prob_grad - row_dot)).astype(jnp.bfloat16)
    query_grad = jnp.einsum(
        "chqk,ckhd->cqhd", score_grad, near_keys, preferred_element_type=jnp.float32
    )
    query_grad = query_grad.astype(jnp.bfloat16).reshape(-1, width_here)
    key_terms = jnp.einsum(
        "chqk,cqhd->ckhd", score_grad, query_blocks, preferred_element_type=jnp.float32
    )
    key_terms = key_terms.reshape(groups * NEIGHBOURS, -1)
    value_terms = jnp.einsum(
        "chqk,cqhd->ckhd", prob_low, cotan_blocks, preferred_element_type=jnp.float32
    )
    value_terms = value_terms.reshape(groups * NEIGHBOURS, -1)
    selector = (jnp.arange(total_rows, dtype=jnp.int32)[:, None] == cache_rows[None, :]).astype(
        jnp.float32
    )
    summed_keys = jnp.dot(
        selector, key_terms, precision=lax.Precision.HIGHEST, preferred_element_type=jnp.float32
    )
    summed_values = jnp.dot(
        selector, value_terms, precision=lax.Precision.HIGHEST, preferred_element_type=jnp.float32
    )
    summed = lax.psum_scatter(
        jnp.concatenate([summed_keys, summed_values], axis=1).astype(jnp.bfloat16),
        "grp",
        scatter_dimension=0,
        tiled=True,
    ).astype(jnp.float32)
    summed = summed.reshape(stored, 2, NEIGH_LEN, width_here)
    attended_back, query_back = (
        lax.all_to_all(attended, "seq", split_axis=0, concat_axis=1, tiled=True),
        lax.all_to_all(query_grad, "seq", split_axis=0, concat_axis=1, tiled=True),
    )
    return (
        attended_back[None],
        query_back[None],
        summed[:, 0].astype(jnp.bfloat16),
        summed[:, 1].astype(jnp.bfloat16),
    )


def solution(mesh):
    placed = (
        P("grp", "seq", None),
        P("grp", "seq", None),
        P("grp", None, "seq"),
        P("grp", None, "seq"),
        P("grp", None, None),
        P(),
    )
    return jax.shard_map(
        on_device,
        mesh=mesh,
        in_specs=placed,
        out_specs=(
            P("grp", "seq", None),
            P("grp", "seq", None),
            P("grp", None, "seq"),
            P("grp", None, "seq"),
        ),
        check_vma=False,
    )
```

profile of v0, /device:TPU:1, one launch (start us, length us, event | category | flops | bytes accessed | tf_op | source)
XLA Modules:
  0.0 365.7 jit_solution(17054618937303615721)
XLA Ops:
  7.2 2.2 copy.39
  9.4 2.7 copy.31
  12.1 13.1 %all-to-all-start = ((bf16[128,64,128]{2,0,1:T(8,128)(2,1)}), bf16[128,64,128]{2,0,1:T(8,128)(2,1)S(1)}, u32[]{:S(2)}, u32[]{:S(2)}) async-start(bf16[128,64,128]{2,0,1:T(8,128)(2,1)} %copy.31), calls=%async_computation | async-start | bytes 4194304 | tf_op jit(solution)/shard_map/all_to_all | solution.py:20
  27.0 2.2 copy.40
  29.2 2.7 copy.33
  31.9 43.0 %all-to-all-done = bf16[128,64,128]{2,0,1:T(8,128)(2,1)S(1)} async-done(((bf16[128,64,128]{2,0,1:T(8,128)(2,1)}), bf16[128,64,128]{2,0,1:T(8,128)(2,1)S(1)}, u32[]{:S(2)}, u32[]{:S(2)}) %all-to-all-start) | async-done | bytes 2097184 | tf_op jit(solution)/shard_map/all_to_all | solution.py:20
  74.9 7.7 %all-to-all-start.2 = ((bf16[128,64,128]{2,0,1:T(8,128)(2,1)}), bf16[128,64,128]{2,0,1:T(8,128)(2,1)}, u32[]{:S(2)}, u32[]{:S(2)}) async-start(bf16[128,64,128]{2,0,1:T(8,128)(2,1)} %copy.33), calls=%async_computation.2 | async-start | bytes 4194304 | tf_op jit(solution)/shard_map/all_to_all | solution.py:21
  82.7 9.8 %gather_fusion = bf16[256,128,128]{2,1,0:T(8,128)(2,1)} fusion(bf16[32,128,128]{2,1,0:T(8,128)(2,1)} %all-gather.3.cloned.1.call-done, s32[1024]{0:T(1024)S(1)} %pad_clamp_fusion), kind=kCustom, calls=%fused_computation.clone | custom fusion | bytes 16778240 | tf_op jit(solution)/shard_map/jit(_take)/gather | solution.py:35
  92.6 9.8 %gather_fusion.1 = bf16[256,128,128]{2,1,0:T(8,128)(2,1)} fusion(bf16[32,128,128]{2,1,0:T(8,128)(2,1)} %all-gather.5.cloned.1.call-done, s32[1024]{0:T(1024)S(1)} %pad_clamp_fusion), kind=kCustom, calls=%fused_computation.1.clone | custom fusion | bytes 16778240 | tf_op jit(solution)/shard_map/jit(_take)/gather | solution.py:32
  102.4 9.5 %broadcast_select_fusion = (bf16[256,128,128]{2,1,0:T(8,128)(2,1)S(1)}, bf16[256,128,128]{2,1,0:T(8,128)(2,1)}) fusion(bf16[256,128,128]{2,1,0:T(8,128)(2,1)} %gather_fusion.1, pred[256]{0:T(512)(128)(4,1)S(1)} %compare_and_fusion, bf16[256,128,128]{2,1,0:T(8,128)(2,1)} %gather_fusion), kind=kLoop, calls=%fused_computation.16 | loop fusion | flops 8388608 | bytes 33554688 | tf_op jit(solution)/shard_map/jit(_take)/select_n | solution.py:32
  111.9 6.3 %fusion.29 = f32[128,256,64]{1,2,0:T(8,128)} fusion(bf16[128,256,128]{2,1,0:T(8,128)(2,1)S(1)} %bitcast.99, bf16[128,64,128]{2,1,0:T(8,128)(2,1)S(1)} %bitcast.101), kind=kOutput, calls=%fused_computation.40 | convolution fusion | flops 536870912 | bytes 18874368 | tf_op jit(solution)/shard_map/cqhd,ckhd->chqk/dot_general | solution.py:40
  118.2 10.7 %fusion.28 = (f32[128,64]{1,0:T(8,128)S(1)}, f32[128,64,256]{2,1,0:T(8,128)}) fusion(f32[128,256,64]{1,2,0:T(8,128)} %fusion.29), kind=kOutput, calls=%fused_computation.39 | output fusion | flops 8388863 | bytes 16809984 | tf_op jit(solution)/shard_map/sub | solution.py:44
  128.9 33.4 %fusion.13 = bf16[128,128,64]{1,2,0:T(8,128)(2,1)} fusion(bf16[128,256,128]{2,1,0:T(8,128)(2,1)} %bitcast.103, f32[128,64]{1,0:T(8,128)S(1)} %get-tuple-element.9, f32[128,256,64]{1,2,0:T(8,128)} %fusion.29), kind=kOutput, calls=%fused_computation.25 | convolution fusion | flops 548413696 | bytes 18907136 | tf_op jit(solution)/shard_map/chqk,ckhd->cqhd/dot_general | solution.py:47
  162.4 10.5 %all-to-all-start.1 = ((bf16[64,128,128]{2,1,0:T(8,128)(2,1)}), bf16[64,128,128]{2,1,0:T(8,128)(2,1)}, u32[]{:S(2)}, u32[]{:S(2)}) async-start(bf16[64,128,128]{2,1,0:T(8,128)(2,1)} %bitcast.110), calls=%async_computation.1 | async-start | bytes 4194304 | tf_op jit(solution)/shard_map/all_to_all | solution.py:86
  172.9 25.9 %convolution_bitcast_fusion = f32[128,256,1,128]{3,1,0,2:T(8,128)} fusion(bf16[128,64,128]{2,1,0:T(8,128)(2,1)} %bitcast.10, f32[128,64]{1,0:T(8,128)S(1)} %get-tuple-element.9, f32[128,256,64]{1,2,0:T(8,128)} %fusion.29), kind=kOutput, calls=%fused_computation.5 | convolution fusion | flops 547365120 | bytes 27295744 | tf_op jit(solution)/shard_map/chqk,cqhd->ckhd/dot_general | solution.py:65
  198.8 10.2 %fusion.1 = (f32[128,64]{1,0:T(8,128)S(1)}, f32[128,256,64]{1,2,0:T(8,128)}) fusion(f32[128,64,256]{2,1,0:T(8,128)} %get-tuple-element.10, f32[128,64]{1,0:T(8,128)S(1)} %get-tuple-element.9, bf16[128,256,128]{2,1,0:T(8,128)(2,1)} %bitcast.104, bf16[128,64,128]{2,1,0:T(8,128)(2,1)} %bitcast.10), kind=kOutput, calls=%fused_computation.9 | convolution fusion | flops 543154176 | bytes 27328512 | tf_op jit(solution)/shard_map/cqhd,ckhd->chqk/dot_general | solution.py:52
  209.0 18.2 %reshape.124 = f32[256,16384]{1,0:T(8,128)} reshape(f32[128,256,1,128]{3,1,0,2:T(8,128)} %convolution_bitcast_fusion) | data formatting | bytes 33554432 | tf_op jit(solution)/shard_map/reshape | solution.py:68
  227.2 10.8 %convolution_convert_fusion = bf16[32,16384]{1,0:T(8,128)(2,1)} fusion(f32[256,16384]{1,0:T(8,128)} %reshape.124, s32[256]{0:T(256)S(1)} %select_reduce_fusion), kind=kOutput, calls=%fused_computation.3 | convolution fusion | flops 1611145216 | bytes 17826816 | tf_op jit(solution)/shard_map/dot_general | solution.py:75
  238.0 6.2 %fusion.3 = bf16[128,64,256]{2,1,0:T(8,128)(2,1)S(1)} fusion(f32[128,256,64]{1,2,0:T(8,128)S(1)} %copy-done.2, f32[128,64]{1,0:T(8,128)S(1)} %get-tuple-element.11, f32[128,64,256]{2,1,0:T(8,128)} %get-tuple-element.10, f32[128,64]{1,0:T(8,128)S(1)} %get-tuple-element.9), kind=kLoop, calls=%fused_computation.11 | loop fusion | flops 10485760 | bytes 21037056 | tf_op jit(solution)/shard_map/convert_element_type | solution.py:56
  244.2 1.9 copy-done.1
  246.1 7.0 %convolution_bitcast_fusion.1 = f32[128,256,1,128]{3,1,0,2:T(8,128)} fusion(bf16[128,64,256]{2,1,0:T(8,128)(2,1)S(1)} %fusion.3, bf16[128,64,128]{2,1,0:T(8,128)(2,1)S(1)} %bitcast.102), kind=kOutput, calls=%fused_computation.6 | convolution fusion | flops 536870912 | bytes 23068672 | tf_op jit(solution)/shard_map/chqk,cqhd->ckhd/dot_general | solution.py:61
  253.2 18.2 %reshape.123 = f32[256,16384]{1,0:T(8,128)} reshape(f32[128,256,1,128]{3,1,0,2:T(8,128)} %convolution_bitcast_fusion.1) | data formatting | bytes 33554432 | tf_op jit(solution)/shard_map/reshape | solution.py:64
  271.4 9.5 %convolution_convert_fusion.1 = bf16[32,16384]{1,0:T(8,128)(2,1)S(1)} fusion(f32[256,16384]{1,0:T(8,128)} %reshape.123, s32[256]{0:T(256)S(1)} %select_reduce_fusion), kind=kOutput, calls=%fused_computation.4 | convolution fusion | flops 1611145216 | bytes 17826816 | tf_op jit(solution)/shard_map/dot_general | solution.py:72
  280.9 1.5 pad_maximum_fusion
  282.4 7.6 %convolution_convert_fusion.2 = bf16[128,128,64]{1,2,0:T(8,128)(2,1)} fusion(bf16[128,64,256]{2,1,0:T(8,128)(2,1)} %copy-done.1, bf16[128,256,128]{2,1,0:T(8,128)(2,1)} %bitcast.100), kind=kOutput, calls=%fused_computation.26 | convolution fusion | flops 537919488 | bytes 14680064 | tf_op jit(solution)/shard_map/chqk,ckhd->cqhd/dot_general | solution.py:57
  290.0 10.5 %all-to-all-start.3 = ((bf16[64,128,128]{2,1,0:T(8,128)(2,1)}), bf16[64,128,128]{2,1,0:T(8,128)(2,1)S(1)}, u32[]{:S(2)}, u32[]{:S(2)}) async-start(bf16[64,128,128]{2,1,0:T(8,128)(2,1)} %bitcast.14), calls=%async_computation.3 | async-start | bytes 4194304 | tf_op jit(solution)/shard_map/all_to_all | solution.py:87
  300.4 4.3 %copy.32 = bf16[128,64,128]{2,1,0:T(8,128)(2,1)} copy(bf16[128,64,128]{2,0,1:T(8,128)(2,1)} %bitcast.8) | data formatting | bytes 4194304 | tf_op jit(solution)/shard_map/all_to_all | solution.py:86
  304.7 4.2 %broadcast_in_dim.36 = bf16[1,128,8192]{2,1,0:T(8,128)(2,1)} reshape(bf16[128,64,128]{2,1,0:T(8,128)(2,1)} %copy.32) | data formatting | bytes 4194304 | tf_op jit(solution)/shard_map/broadcast_in_dim | solution.py:90
  308.9 41.3 %all-to-all-done.3 = bf16[64,128,128]{2,1,0:T(8,128)(2,1)S(1)} async-done(((bf16[64,128,128]{2,1,0:T(8,128)(2,1)}), bf16[64,128,128]{2,1,0:T(8,128)(2,1)S(1)}, u32[]{:S(2)}, u32[]{:S(2)}) %all-to-all-start.3) | async-done | bytes 2097184 | tf_op jit(solution)/shard_map/all_to_all | solution.py:87
  350.2 2.7 copy.34
  352.9 4.2 %broadcast_in_dim.37 = bf16[1,128,8192]{2,1,0:T(8,128)(2,1)} reshape(bf16[128,64,128]{2,1,0:T(8,128)(2,1)} %copy.34) | data formatting | bytes 4194304 | tf_op jit(solution)/shard_map/broadcast_in_dim | solution.py:91
  357.0 1.1 fusion.27
  (29 shorter events, 2.8 us)
Async XLA Ops:
  7.2 19.5 %copy-start.4 = (s32[1,128,2]{1,2,0:T(2,128)S(1)}, s32[1,128,2]{1,2,0:T(2,128)}, u32[]{:S(2)}) copy-start(s32[1,128,2]{1,2,0:T(2,128)} %param.12) | copy-start | bytes 3076
  9.4 22.5 %copy-start.5 = (s32[32]{0:T(128)S(1)}, s32[32]{0:T(128)}, u32[]{:S(2)}) copy-start(s32[32]{0:T(128)} %param.13) | copy-start | bytes 388
  12.1 62.9 %all-to-all-start = ((bf16[128,64,128]{2,0,1:T(8,128)(2,1)}), bf16[128,64,128]{2,0,1:T(8,128)(2,1)S(1)}, u32[]{:S(2)}, u32[]{:S(2)}) async-start(bf16[128,64,128]{2,0,1:T(8,128)(2,1)} %copy.31), calls=%async_computation | async-start | bytes 4194304 | tf_op jit(solution)/shard_map/all_to_all | solution.py:20
  25.2 57.5 %all-gather.3.cloned.1.call-start = ((), (), s32[]{:S(2)}) async-start(), calls=%async_computation.5 | async-start | bytes 1310720 | tf_op jit(solution)/shard_map/all_gather | solution.py:29
  25.9 66.6 %all-gather.5.cloned.1.call-start = ((), (), s32[]{:S(2)}) async-start(), calls=%async_computation.6 | async-start | bytes 1310720 | tf_op jit(solution)/shard_map/all_gather | solution.py:28
  74.9 87.5 %all-to-all-start.2 = ((bf16[128,64,128]{2,0,1:T(8,128)(2,1)}), bf16[128,64,128]{2,0,1:T(8,128)(2,1)}, u32[]{:S(2)}, u32[]{:S(2)}) async-start(bf16[128,64,128]{2,0,1:T(8,128)(2,1)} %copy.33), calls=%async_computation.2 | async-start | bytes 4194304 | tf_op jit(solution)/shard_map/all_to_all | solution.py:21
  111.9 6.3 %copy-start = (bf16[256,128,128]{2,1,0:T(8,128)(2,1)}, bf16[256,128,128]{2,1,0:T(8,128)(2,1)S(1)}, u32[]{:S(2)}) copy-start(bf16[256,128,128]{2,1,0:T(8,128)(2,1)S(1)} %get-tuple-element.7) | copy-start | bytes 25165828
  162.4 127.6 %all-to-all-start.1 = ((bf16[64,128,128]{2,1,0:T(8,128)(2,1)}), bf16[64,128,128]{2,1,0:T(8,128)(2,1)}, u32[]{:S(2)}, u32[]{:S(2)}) async-start(bf16[64,128,128]{2,1,0:T(8,128)(2,1)} %bitcast.110), calls=%async_computation.1 | async-start | bytes 4194304 | tf_op jit(solution)/shard_map/all_to_all | solution.py:86
  172.9 184.1 %reduce-scatter.2.cloned.1.call-start = ((), (), s32[]{:S(2)}) async-start(), calls=%async_computation.7 | async-start | bytes 2621440 | tf_op jit(solution)/shard_map/reduce_scatter | solution.py:78
  227.2 10.8 %copy-start.2 = (f32[128,256,64]{1,2,0:T(8,128)S(1)}, f32[128,256,64]{1,2,0:T(8,128)}, u32[]{:S(2)}) copy-start(f32[128,256,64]{1,2,0:T(8,128)} %get-tuple-element.12) | copy-start | bytes 25165828
  244.2 1.9 copy-start.1
  271.4 9.5 %copy-start.3 = (bf16[32,16384]{1,0:T(8,128)(2,1)S(1)}, bf16[32,16384]{1,0:T(8,128)(2,1)}, u32[]{:S(2)}) copy-start(bf16[32,16384]{1,0:T(8,128)(2,1)} %convolution_convert_fusion) | copy-start | bytes 3145732
  290.0 60.2 %all-to-all-start.3 = ((bf16[64,128,128]{2,1,0:T(8,128)(2,1)}), bf16[64,128,128]{2,1,0:T(8,128)(2,1)S(1)}, u32[]{:S(2)}, u32[]{:S(2)}) async-start(bf16[64,128,128]{2,1,0:T(8,128)(2,1)} %bitcast.14), calls=%async_computation.3 | async-start | bytes 4194304 | tf_op jit(solution)/shard_map/all_to_all | solution.py:87
Sparse Core Ops, SparseCore 0:
  27.8 25.6 all-gather.2
  55.3 26.8 all-gather.4
  282.5 33.1 reduce-scatter.1
where the time goes:
time: 373 us; the launch traced here: 366 us
  matrix products  111 us (30%)
  waiting for transfers between devices  85.7 us (23%)
  local copies, waits for them, and re-layouts  85.2 us (23%)
  starting transfers between devices  41.9 us (11%)
  other arithmetic  28.1 us (8%)
  between operations  14.1 us (4%)
    all_to_all x1, waiting for transfers between devices, on_device(): lax.all_to_all(queries[0], 'seq', split_axis=1, concat_axis=0, tiled=True)  43 us
    all_to_all x1, waiting for transfers between devices, on_device(): lax.all_to_all(query_grad, 'seq', split_axis=0, concat_axis=1, tiled=True)  41.3 us
    dot_general x1, matrix products, on_device(): jnp.einsum('chqk,ckhd->cqhd', prob_low, near_values, preferred_element_ty...  33.4 us
    dot_general x1, matrix products, on_device(): jnp.einsum('chqk,cqhd->ckhd', prob_low, cotan_blocks, preferred_element_t...  25.9 us
    reshape x1, local copies, waits for them, and re-layouts, on_device(): key_terms = key_terms.reshape(groups * NEIGHBOURS, -1)  18.2 us
    reshape x1, local copies, waits for them, and re-layouts, on_device(): value_terms = value_terms.reshape(groups * NEIGHBOURS, -1)  18.2 us
    all_to_all x1, starting transfers between devices, on_device(): lax.all_to_all(queries[0], 'seq', split_axis=1, concat_axis=0, tiled=True)  13.1 us
    dot_general x1, matrix products, on_device(): jnp.dot(selector, value_terms, precision=lax.Precision.HIGHEST, preferred...  10.8 us
  transfers between devices with their start and end apart: 7, of which 2 were waited for; matrix products, arithmetic and copies ran while one was open for 59% of the time, Pallas kernels for 0%

commit v1 on v0

v1 whole, which is shorter than its diff:
```python
import functools
import math

import jax
import jax.numpy as jnp
from jax import lax
from jax.experimental import pallas as pl
from jax.experimental.pallas import tpu as pltpu
from jax.sharding import PartitionSpec as P

HEAD_DIM = 128
GROUP = 64
NEIGH_LEN = 128
MESH = pl.DeviceIdType.MESH
ZS, YS, CS, XS = 8, 4, 2, 4
SRC = 32
TOKENS = 128
ROWS = 8
STORED = ROWS * XS
ITEMS = SRC * 4
ZERO = ITEMS


def offsets(i):
    return i % 4, (i // 4) % 4, i // 16


def kernel(
    rows_ref, prev_ref, last_ref, q_ref, g_ref, ck_ref, cv_ref,
    out_ref, grad_ref,
    rbuf, obuf, ka, va, kb, vb, tk, tv, dsend, drecv, krelay, bsend, brelay, bfinal,
    in_send, in_recv, out_send, out_recv, own_sem, ag_send, ag_recv, zs_send, zs_recv, rs_send, rs_recv, bz_send, bz_recv,
):
    scale = 1.0 / math.sqrt(HEAD_DIM)
    seq = lax.axis_index("seq")
    x = lax.axis_index("grp")
    z, y, c = seq // (YS * CS), (seq // CS) % YS, seq % CS
    right, left = (x + 1) % XS, (x + XS - 1) % XS

    def at(zz, yy, cc):
        return (zz * YS + yy) * CS + cc

    z_next = at((z + 2 + 4 * c) % ZS, y, c)

    def source(i):
        k, dy, dc = offsets(i)
        return at((z + k + ZS - 1 - c) % ZS, (y + dy) % YS, (c + dc) % CS)

    def dest(i):
        k, dy, dc = offsets(i)
        cc = (c + dc) % CS
        return at((z - k + ZS + 1 + cc) % ZS, (y - dy + YS) % YS, cc)

    def head_of(device, which):
        return (device + which * (ZS // 2) * YS * CS) % (ZS * YS * CS)

    def columns(head):
        return pl.ds(pl.multiple_of(head * HEAD_DIM, HEAD_DIM), HEAD_DIM)

    barrier = pltpu.get_barrier_semaphore()

    def greet(n, carry):
        zz = (z + ZS - 2 + n // (YS * CS)) % ZS
        peer = at(zz, (n // CS) % YS, n % CS)

        @pl.when(peer != seq)
        def _():
            pl.semaphore_signal(barrier, inc=1, device_id=(peer, x), device_id_type=MESH)

        return carry

    lax.fori_loop(0, 5 * YS * CS, greet, 0)
    for o in range(1, XS):
        pl.semaphore_signal(barrier, inc=1, device_id=(seq, (x + o) % XS), device_id_type=MESH)
    pl.semaphore_wait(barrier, 5 * YS * CS - 1 + XS - 1)

    def remote(src, dst, send, recv, device):
        return pltpu.make_async_remote_copy(
            src_ref=src, dst_ref=dst, send_sem=send, recv_sem=recv, device_id=device, device_id_type=MESH
        )

    def block(owner):
        return pl.ds(pl.multiple_of(owner * ROWS, ROWS), ROWS)

    mine = block(x)
    caches = ((ka, va), (kb, vb))

    def gather_first(which, srcs):
        copies = []
        for kv in range(2):
            dst = caches[which][kv].at[mine]
            copies.append(remote(srcs[kv], dst, ag_send.at[which, 0, kv], ag_recv.at[which, 0, kv], (seq, right)))
            copies.append(remote(srcs[kv], dst, ag_send.at[which, 1, kv], ag_recv.at[which, 1, kv], (seq, left)))
        return copies

    def gather_second(which):
        near = caches[which]
        from_left, from_right = near[0].at[block(left)], near[1].at[block(right)]
        return [
            remote(from_left, from_left, ag_send.at[which, 2, 0], ag_recv.at[which, 2, 0], (seq, right)),
            remote(from_right, from_right, ag_send.at[which, 2, 1], ag_recv.at[which, 2, 1], (seq, left)),
        ]

    own = [
        pltpu.make_async_copy(ck_ref, ka.at[mine], own_sem.at[0]),
        pltpu.make_async_copy(cv_ref, va.at[mine], own_sem.at[1]),
    ]
    gather_a = gather_first(0, (ck_ref, cv_ref))
    shift_first = [
        remote(src, krelay.at[kv], zs_send.at[0, kv], zs_recv.at[0, kv], (z_next, x))
        for kv, src in enumerate((ck_ref, cv_ref))
    ]
    shift_second = [
        remote(krelay.at[kv], caches[1][kv].at[mine], zs_send.at[1, kv], zs_recv.at[1, kv], (z_next, x))
        for kv in range(2)
    ]
    for copy in own + shift_first + gather_a:
        copy.start()

    def in_copies(which, i):
        device = dest(i)
        cols = columns(head_of(device, which))
        return [
            (src.at[:, cols], rbuf.at[which, i, n], in_send.at[which, i], in_recv.at[which, i], (device, x))
            for n, src in enumerate((q_ref, g_ref))
        ]

    def send_in(which):
        def step(i, carry):
            here = dest(i) == seq

            @pl.when(here)
            def _():
                for src, dst, _send, recv, _device in in_copies(which, i):
                    pltpu.make_async_copy(src, dst, recv).start()

            @pl.when(jnp.logical_not(here))
            def _():
                for args in in_copies(which, i):
                    remote(*args).start()

            return carry

        lax.fori_loop(0, SRC, step, 0)

    send_in(0)
    for kv in range(2):
        shift_first[kv].wait_recv()
        shift_second[kv].start()
    gather_a2 = gather_second(0)
    for copy in gather_a:
        copy.wait_recv()
    for copy in gather_a2:
        copy.start()
    send_in(1)

    tk[ZERO] = jnp.zeros((HEAD_DIM, NEIGH_LEN), jnp.float32)
    tv[ZERO] = jnp.zeros((HEAD_DIM, NEIGH_LEN), jnp.float32)
    for copy in own:
        copy.wait()
    for copy in gather_a2:
        copy.wait_recv()

    def nt(a, b):
        return lax.dot_general(a, b, (((1,), (1,)), ((), ())), preferred_element_type=jnp.float32)

    def nn(a, b):
        return lax.dot_general(a, b, (((1,), (0,)), ((), ())), preferred_element_type=jnp.float32)

    def tn(a, b):
        return lax.dot_general(a, b, (((0,), (0,)), ((), ())), preferred_element_type=jnp.float32)

    def attend(which, i):
        kref, vref = caches[which]
        first = source(i) * 4
        for g in range(2):
            span = pl.ds(g * GROUP, GROUP)
            r0, r1 = rows_ref[first + 2 * g], rows_ref[first + 2 * g + 1]
            q = rbuf[which, i, 0, span, :]
            ct = rbuf[which, i, 1, span, :]
            keys = jnp.concatenate([kref[r0], kref[r1]], axis=0)
            vals = jnp.concatenate([vref[r0], vref[r1]], axis=0)
            raw = nt(q, keys)
            weights = jnp.exp((raw - jnp.max(raw, axis=-1, keepdims=True)) * scale)
            prob = weights * (1.0 / jnp.sum(weights, axis=-1, keepdims=True))
            low = prob.astype(jnp.bfloat16)
            obuf[which, i, 0, span, :] = nn(low, vals).astype(jnp.bfloat16)
            pg = nt(ct, vals)
            dot = jnp.sum(prob * pg, axis=-1, keepdims=True)
            sg = (scale * prob * (pg - dot)).astype(jnp.bfloat16)
            obuf[which, i, 1, span, :] = nn(sg, keys).astype(jnp.bfloat16)
            kt = tn(q, sg)
            vt = tn(ct, low)
            for j in range(2):
                before = prev_ref[first + 2 * g + j]
                lanes = slice(j * NEIGH_LEN, (j + 1) * NEIGH_LEN)
                tk[i * 4 + 2 * g + j] = tk[before] + kt[:, lanes]
                tv[i * 4 + 2 * g + j] = tv[before] + vt[:, lanes]

    def send_out(which, i):
        device = source(i)
        cols = columns(head_of(seq, which))
        here = device == seq

        @pl.when(here)
        def _():
            pltpu.make_async_copy(obuf.at[which, i], out_ref.at[:, :, cols], out_recv.at[which, i]).start()

        @pl.when(jnp.logical_not(here))
        def _():
            remote(
                obuf.at[which, i], out_ref.at[:, :, cols], out_send.at[which, i], out_recv.at[which, i], (device, x)
            ).start()

    def compute(which, begin, end):
        def step(i, carry):
            pltpu.make_async_copy(obuf.at[which, i], rbuf.at[which, i], in_recv.at[which, i]).wait()
            attend(which, i)

            @pl.when(i > 0)
            def _():
                send_out(which, i - 1)

            return carry

        lax.fori_loop(begin, end, step, 0)

    def reduce_out(which):
        def step(r, carry):
            slot = last_ref[r]
            dsend[which, r // ROWS, 0, r % ROWS] = tk[slot].astype(jnp.bfloat16)
            dsend[which, r // ROWS, 1, r % ROWS] = tv[slot].astype(jnp.bfloat16)
            return carry

        lax.fori_loop(0, STORED, step, 0)
        send_out(which, SRC - 1)
        copies = []
        for o in range(1, XS):
            xd = (x + o) % XS
            copies.append(
                remote(
                    dsend.at[which, xd], drecv.at[which, o - 1], rs_send.at[which, o - 1], rs_recv.at[which, o - 1],
                    (seq, xd),
                )
            )
        for copy in copies:
            copy.start()
        return copies

    def summed(which, kv, r):
        total = dsend[which, x, kv, r].astype(jnp.float32)
        for o in range(XS - 1):
            total = total + drecv[which, o, kv, r].astype(jnp.float32)
        return total

    compute(0, 0, 8)
    for copy in shift_second:
        copy.wait_recv()
    gather_b = gather_first(1, (kb.at[mine], vb.at[mine]))
    for copy in gather_b:
        copy.start()
    compute(0, 8, 20)
    gather_b2 = gather_second(1)
    for copy in gather_b:
        copy.wait_recv()
    for copy in gather_b2:
        copy.start()
    compute(0, 20, SRC)
    scatter_a = reduce_out(0)
    for copy in gather_b2:
        copy.wait_recv()
    compute(1, 0, SRC)
    scatter_b = reduce_out(1)

    for copy in scatter_b:
        copy.wait_recv()

    def far(n, carry):
        kv, r = n // ROWS, n % ROWS
        bsend[kv, r] = summed(1, kv, r).astype(jnp.bfloat16)
        return carry

    lax.fori_loop(0, 2 * ROWS, far, 0)
    back_first = remote(bsend, brelay, bz_send.at[0], bz_recv.at[0], (z_next, x))
    back_second = remote(brelay, bfinal, bz_send.at[1], bz_recv.at[1], (z_next, x))
    back_first.start()
    for copy in scatter_a:
        copy.wait_recv()
    back_first.wait_recv()
    back_second.start()
    back_second.wait_recv()

    def near(n, carry):
        kv, r = n // ROWS, n % ROWS
        total = summed(0, kv, r) + bfinal[kv, r].astype(jnp.float32)
        grad_ref[kv, r] = total.T.astype(jnp.bfloat16)
        return carry

    lax.fori_loop(0, 2 * ROWS, near, 0)

    def drain(which):
        def step(i, carry):
            pltpu.make_async_copy(obuf.at[which, i], out_ref.at[:, :, columns(0)], out_recv.at[which, i]).wait()

            @pl.when(dest(i) != seq)
            def _():
                remote(
                    obuf.at[which, i], rbuf.at[which, i], in_send.at[which, i], in_recv.at[which, i], (dest(i), x)
                ).wait_send()

            @pl.when(source(i) != seq)
            def _():
                remote(
                    obuf.at[which, i], out_ref.at[:, :, columns(0)], out_send.at[which, i], out_recv.at[which, i],
                    (source(i), x),
                ).wait_send()

            return carry

        lax.fori_loop(0, SRC, step, 0)

    for copy in (
        shift_first + shift_second + gather_a + gather_a2 + gather_b + gather_b2 + scatter_a + scatter_b
        + [back_first, back_second]
    ):
        copy.wait_send()
    drain(0)
    drain(1)


def on_device(queries, cotangent, cache_keys, cache_values, block_table, block_slot):
    seq = lax.axis_index("seq")
    z, y, c = seq // (YS * CS), (seq // CS) % YS, seq % CS
    flat = block_table[0].reshape(-1)
    blocks = block_slot.shape[0]
    hit = flat[:, None] == jnp.arange(blocks, dtype=jnp.int32)[None, :]
    rows = jnp.sum(jnp.where(hit, block_slot[None, :], 0), axis=1)
    item = jnp.arange(flat.shape[0], dtype=jnp.int32)
    src = item // 4
    k = (src // (YS * CS) - z + 1 + c + ZS) % ZS
    step = ((src % CS - c + CS) % CS) * 16 + (((src // CS) % YS - y + YS) % YS) * 4 + k
    slot = jnp.where(k < 4, step * 4 + item % 4, -1)
    same = (rows[:, None] == rows[None, :]) & (slot[None, :] < slot[:, None])
    before = jnp.max(jnp.where(same, slot[None, :], -1), axis=1)
    before = jnp.where(before < 0, ZERO, before)
    final = jnp.max(jnp.where(rows[None, :] == jnp.arange(STORED, dtype=jnp.int32)[:, None], slot[None, :], -1), axis=1)
    final = jnp.where(final < 0, ZERO, final)
    smem = pl.BlockSpec(memory_space=pltpu.SMEM)
    hbm = pl.BlockSpec(memory_space=pl.ANY)
    bf16 = jnp.bfloat16
    dma = pltpu.SemaphoreType.DMA
    out, grads = pl.pallas_call(
        kernel,
        out_shape=(
            jax.ShapeDtypeStruct((2, TOKENS, queries.shape[2]), bf16),
            jax.ShapeDtypeStruct((2, ROWS, NEIGH_LEN, HEAD_DIM), bf16),
        ),
        in_specs=[smem, smem, smem, hbm, hbm, hbm, hbm],
        out_specs=(hbm, pl.BlockSpec(memory_space=pltpu.VMEM)),
        scratch_shapes=[
            pltpu.VMEM((2, SRC, 2, TOKENS, HEAD_DIM), bf16),
            pltpu.VMEM((2, SRC, 2, TOKENS, HEAD_DIM), bf16),
            pltpu.VMEM((STORED, NEIGH_LEN, HEAD_DIM), bf16),
            pltpu.VMEM((STORED, NEIGH_LEN, HEAD_DIM), bf16),
            pltpu.VMEM((STORED, NEIGH_LEN, HEAD_DIM), bf16),
            pltpu.VMEM((STORED, NEIGH_LEN, HEAD_DIM), bf16),
            pltpu.VMEM((ITEMS + 1, HEAD_DIM, NEIGH_LEN), jnp.float32),
            pltpu.VMEM((ITEMS + 1, HEAD_DIM, NEIGH_LEN), jnp.float32),
            pltpu.VMEM((2, XS, 2, ROWS, HEAD_DIM, NEIGH_LEN), bf16),
            pltpu.VMEM((2, XS - 1, 2, ROWS, HEAD_DIM, NEIGH_LEN), bf16),
            pltpu.VMEM((2, ROWS, NEIGH_LEN, HEAD_DIM), bf16),
            pltpu.VMEM((2, ROWS, HEAD_DIM, NEIGH_LEN), bf16),
            pltpu.VMEM((2, ROWS, HEAD_DIM, NEIGH_LEN), bf16),
            pltpu.VMEM((2, ROWS, HEAD_DIM, NEIGH_LEN), bf16),
            dma((2, SRC)), dma((2, SRC)), dma((2, SRC)), dma((2, SRC)),
            dma((2,)), dma((2, 3, 2)), dma((2, 3, 2)), dma((2, 2)), dma((2, 2)),
            dma((2, XS - 1)), dma((2, XS - 1)), dma((2,)), dma((2,)),
        ],
        compiler_params=pltpu.CompilerParams(
            collective_id=0, has_side_effects=True, vmem_limit_bytes=60 * 1024 * 1024
        ),
        name="retrieval_attention",
    )(rows, before, final, queries[0], cotangent[0], cache_keys, cache_values)
    return out[0][None], out[1][None], grads[0], grads[1]


def solution(mesh):
    placed = (
        P("grp", "seq", None),
        P("grp", "seq", None),
        P("grp", None, "seq"),
        P("grp", None, "seq"),
        P("grp", None, None),
        P(),
    )
    return jax.shard_map(
        on_device,
        mesh=mesh,
        in_specs=placed,
        out_specs=(
            P("grp", "seq", None),
            P("grp", "seq", None),
            P("grp", None, "seq"),
            P("grp", None, "seq"),
        ),
        check_vma=False,
    )
```

time: 373 us -> 213 us (0.57); the launches traced: 366 us -> 210 us
  Pallas kernels: 0 us -> 201 us
  matrix products: 111 us -> 0 us
  waiting for transfers between devices: 85.7 us -> 0 us
  local copies, waits for them, and re-layouts: 85.2 us -> 6.5 us
  starting transfers between devices: 41.9 us -> 0 us
  other arithmetic: 28.1 us -> 2.19 us
  between operations: 14.1 us -> 0.7 us
    pallas_call x0 -> x1, Pallas kernels: none -> 201 us  [on_device(): pl.pallas_call(kernel, out_shape=(jax.ShapeDtypeStruct((2, TOKENS, querie...]
    dot_general x8 -> x0, matrix products: 111 us -> none  [the longest x1 33.4 us: on_device(): jnp.einsum('chqk,ckhd->cqhd', prob_low, near_values, preferred_element_ty...]
    all_to_all x4 -> x0, waiting for transfers between devices: 84.3 us -> none  [the longest x1 43 us: on_device(): lax.all_to_all(queries[0], 'seq', split_axis=1, concat_axis=0, tiled=True)]
    all_to_all x4 -> x0, starting transfers between devices: 41.8 us -> none  [the longest x1 13.1 us: on_device(): lax.all_to_all(queries[0], 'seq', split_axis=1, concat_axis=0, tiled=True)]
    reshape x2 -> x0, local copies, waits for them, and re-layouts: 36.4 us -> none  [the longest x1 18.2 us: on_device(): key_terms = key_terms.reshape(groups * NEIGHBOURS, -1)]
    gather x2 -> x0, local copies, waits for them, and re-layouts: 19.7 us -> none  [the longest x1 9.84 us: on_device(): jnp.take(whole_values, cache_rows, axis=0)]
    all_to_all x4 -> x0, local copies, waits for them, and re-layouts: 12.3 us -> none  [the longest x1 4.28 us: on_device(): lax.all_to_all(attended, 'seq', split_axis=0, concat_axis=1, tiled=True)]
    sub x1 -> x0, other arithmetic: 10.7 us -> none  [on_device(): weights = jnp.exp(scores - row_max)]
  transfers between devices with their start and end apart: 7 -> 0, of which waited for: 2 -> 0; matrix products, arithmetic and copies ran while one was open for 59% -> 0% of each run, Pallas kernels for 0% -> 0%
where the time goes in v1:
time: 213 us; the launch traced here: 210 us
  Pallas kernels  201 us (94%)
  local copies, waits for them, and re-layouts  6.5 us (3%)
  other arithmetic  2.19 us (1%)
    pallas_call x1, Pallas kernels, on_device(): pl.pallas_call(kernel, out_shape=(jax.ShapeDtypeStruct((2, TOKENS, querie...  201 us
    slice x1, local copies, waits for them, and re-layouts, on_device(): return (out[0][None], out[1][None], grads[0], grads[1])  4.73 us

profile of v1, /device:TPU:1, one launch (start us, length us, event | category | flops | bytes accessed | tf_op | source)
XLA Modules:
  0.0 210.2 jit_solution(5339821082601114333)
XLA Ops:
  0.7 0.8 copy.11
  1.5 0.1 eq.51
  1.6 0.7 select_reduce_fusion.2.rows_ref
  2.4 0.0 copy-start.1
  2.4 0.1 select_reduce_fusion.1
  2.5 0.2 select_reduce_fusion
  2.7 0.6 compare_select_fusion.prev_ref
  3.3 0.5 compare_select_fusion.1.last_ref
  3.8 0.0 copy-done.1
  3.8 200.9 %retrieval_attention.1 = (bf16[2,128,8192]{2,1,0:T(8,128)(2,1)}, bf16[2,8,128,128]{3,2,1,0:T(8,128)(2,1)}) custom-call(s32[256]{0:T(256)} %copy-done.1, s32[256]{0:T(256)} %compare_select_fusion.prev_ref, s32[32]{0:T(128)} %compare_select_fusion.1.last_ref, bf16[128,8192]{1,0:T(8,128)(2,1)} %bitcast.6, bf16[128,8192]{1,0:T(8,128)(2,1)} %bitcast.7, ...), custom_call_target="tpu_custom_call" | custom-call | tf_op jit(solution)/shard_map/retrieval_attention/pallas_call | solution.py:352
  204.7 0.0 copy-start
  204.7 4.7 %fusion.14 = (bf16[1,128,8192]{2,1,0:T(8,128)(2,1)}, bf16[1,128,8192]{2,1,0:T(8,128)(2,1)}) fusion(bf16[2,128,8192]{2,1,0:T(8,128)(2,1)} %get-tuple-element.6), kind=kLoop, calls=%fused_computation.49 | loop fusion | bytes 8388608 | tf_op jit(solution)/shard_map/slice | solution.py:384
  209.4 0.0 copy-done
  209.4 0.8 slice_bitcast_fusion
  (1 shorter events, 0.0 us)
Async XLA Ops:
  2.4 1.4 copy-start.1
  204.7 4.7 %copy-start = (bf16[2,8,128,128]{3,2,1,0:T(8,128)(2,1)S(1)}, bf16[2,8,128,128]{3,2,1,0:T(8,128)(2,1)}, u32[]{:S(2)}) copy-start(bf16[2,8,128,128]{3,2,1,0:T(8,128)(2,1)} %get-tuple-element.7) | copy-start | bytes 1572868

commit v2 on v1

--- a/solution.py
+++ b/solution.py
@@ -18,17 +18,20 @@
 ROWS = 8
 STORED = ROWS * XS
 ITEMS = SRC * 4
+FIRST = 16
 ZERO = ITEMS
 
 
 def offsets(i):
-    return i % 4, (i // 4) % 4, i // 16
+    other = (i + 24) // 32
+    n = i * (1 - other) + other * ((i + 16) // 3 - 8)
+    return other * (1 + (i + 1) % 3), n % 4, n // 4
 
 
 def kernel(
     rows_ref, prev_ref, last_ref, q_ref, g_ref, ck_ref, cv_ref,
     out_ref, grad_ref,
-    rbuf, obuf, ka, va, kb, vb, tk, tv, dsend, drecv, krelay, bsend, brelay, bfinal,
+    rbuf, obuf, ka, va, kb, vb, tka, tva, tkb, tvb, dsend, dfar, dnear, dsum, dring, krelay, bsend, brelay, bfinal,
     in_send, in_recv, out_send, out_recv, own_sem, ag_send, ag_recv, zs_send, zs_recv, rs_send, rs_recv, bz_send, bz_recv,
 ):
     scale = 1.0 / math.sqrt(HEAD_DIM)
@@ -43,13 +46,13 @@
     z_next = at((z + 2 + 4 * c) % ZS, y, c)
 
     def source(i):
-        k, dy, dc = offsets(i)
-        return at((z + k + ZS - 1 - c) % ZS, (y + dy) % YS, (c + dc) % CS)
+        j, dy, dc = offsets(i)
+        return at((z + (j + 1 + c) % 4 + ZS - 1 - c) % ZS, (y + dy) % YS, (c + dc) % CS)
 
     def dest(i):
-        k, dy, dc = offsets(i)
+        j, dy, dc = offsets(i)
         cc = (c + dc) % CS
-        return at((z - k + ZS + 1 + cc) % ZS, (y - dy + YS) % YS, cc)
+        return at((z - (j + 1 + cc) % 4 + ZS + 1 + cc) % ZS, (y - dy + YS) % YS, cc)
 
     def head_of(device, which):
         return (device + which * (ZS // 2) * YS * CS) % (ZS * YS * CS)
@@ -84,6 +87,7 @@
 
     mine = block(x)
     caches = ((ka, va), (kb, vb))
+    terms = ((tka, tva), (tkb, tvb))
 
     def gather_first(which, srcs):
         copies = []
@@ -114,7 +118,7 @@
         remote(krelay.at[kv], caches[1][kv].at[mine], zs_send.at[1, kv], zs_recv.at[1, kv], (z_next, x))
         for kv in range(2)
     ]
-    for copy in own + shift_first + gather_a:
+    for copy in shift_first + gather_a + own:
         copy.start()
 
     def in_copies(which, i):
@@ -125,7 +129,7 @@
             for n, src in enumerate((q_ref, g_ref))
         ]
 
-    def send_in(which):
+    def send_in(which, begin, end):
         def step(i, carry):
             here = dest(i) == seq
 
@@ -141,21 +145,23 @@
 
             return carry
 
-        lax.fori_loop(0, SRC, step, 0)
-
-    send_in(0)
+        lax.fori_loop(begin, end, step, 0)
+
+    send_in(0, 0, 8)
     for kv in range(2):
         shift_first[kv].wait_recv()
         shift_second[kv].start()
+    send_in(0, 8, FIRST)
     gather_a2 = gather_second(0)
     for copy in gather_a:
         copy.wait_recv()
     for copy in gather_a2:
         copy.start()
-    send_in(1)
-
-    tk[ZERO] = jnp.zeros((HEAD_DIM, NEIGH_LEN), jnp.float32)
-    tv[ZERO] = jnp.zeros((HEAD_DIM, NEIGH_LEN), jnp.float32)
+    send_in(1, 0, SRC)
+    send_in(0, FIRST, SRC)
+
+    for ref in (tka, tva, tkb, tvb):
+        ref[ZERO] = jnp.zeros((HEAD_DIM, NEIGH_LEN), jnp.float32)
     for copy in own:
         copy.wait()
     for copy in gather_a2:
@@ -172,6 +178,7 @@
 
     def attend(which, i):
         kref, vref = caches[which]
+        tk, tv = terms[which]
         first = source(i) * 4
         for g in range(2):
             span = pl.ds(g * GROUP, GROUP)
@@ -212,12 +219,12 @@
                 obuf.at[which, i], out_ref.at[:, :, cols], out_send.at[which, i], out_recv.at[which, i], (device, x)
             ).start()
 
-    def compute(which, begin, end):
+    def compute(which, begin, end, first):
         def step(i, carry):
             pltpu.make_async_copy(obuf.at[which, i], rbuf.at[which, i], in_recv.at[which, i]).wait()
             attend(which, i)
 
-            @pl.when(i > 0)
+            @pl.when(i > first)
             def _():
                 send_out(which, i - 1)
 
@@ -225,7 +232,18 @@
 
         lax.fori_loop(begin, end, step, 0)
 
-    def reduce_out(which):
+    def add(refs):
+        total = refs[0][...].astype(jnp.float32)
+        for ref in refs[1:]:
+            total = total + ref[...].astype(jnp.float32)
+        return total
+
+    far_owner = (x + 2) % XS
+    toward, away = (right, left), (left, right)
+
+    def scatter_first(which):
+        tk, tv = terms[which]
+
         def step(r, carry):
             slot = last_ref[r]
             dsend[which, r // ROWS, 0, r % ROWS] = tk[slot].astype(jnp.bfloat16)
@@ -233,46 +251,71 @@
             return carry
 
         lax.fori_loop(0, STORED, step, 0)
-        send_out(which, SRC - 1)
         copies = []
-        for o in range(1, XS):
-            xd = (x + o) % XS
+        for kv in range(2):
             copies.append(
                 remote(
-                    dsend.at[which, xd], drecv.at[which, o - 1], rs_send.at[which, o - 1], rs_recv.at[which, o - 1],
-                    (seq, xd),
+                    dsend.at[which, far_owner, kv], dfar.at[which, kv], rs_send.at[which, 0, kv], rs_recv.at[which, 0, kv],
+                    (seq, toward[kv]),
                 )
             )
+        for kv in range(2):
+            copies.append(
+                remote(
+                    dsend.at[which, away[kv], kv], dnear.at[which, kv], rs_send.at[which, 1, kv], rs_recv.at[which, 1, kv],
+                    (seq, away[kv]),
+                )
+            )
+        return copies
+
+    def scatter_second(which, first_copies):
+        copies = []
+        for kv in range(2):
+            first_copies[kv].wait_recv()
+
+            def step(r, carry, kv=kv):
+                dsum[which, kv, r] = add((dsend.at[which, toward[kv], kv, r], dfar.at[which, kv, r])).astype(jnp.bfloat16)
+                return carry
+
+            lax.fori_loop(0, ROWS, step, 0)
+            copies.append(
+                remote(
+                    dsum.at[which, kv], dring.at[which, kv], rs_send.at[which, 2, kv], rs_recv.at[which, 2, kv],
+                    (seq, toward[kv]),
+                )
+            )
+        return copies
+
+    def summed(which, kv, r):
+        return add((dsend.at[which, x, kv, r], dnear.at[which, kv, r], dring.at[which, kv, r]))
+
+    def start(copies):
         for copy in copies:
             copy.start()
-        return copies
-
-    def summed(which, kv, r):
-        total = dsend[which, x, kv, r].astype(jnp.float32)
-        for o in range(XS - 1):
-            total = total + drecv[which, o, kv, r].astype(jnp.float32)
-        return total
-
-    compute(0, 0, 8)
+
+    compute(0, 0, 5, 0)
     for copy in shift_second:
         copy.wait_recv()
     gather_b = gather_first(1, (kb.at[mine], vb.at[mine]))
-    for copy in gather_b:
-        copy.start()
-    compute(0, 8, 20)
+    start(gather_b)
+    compute(0, 5, 11, 0)
     gather_b2 = gather_second(1)
     for copy in gather_b:
         copy.wait_recv()
+    start(gather_b2)
+    compute(0, 11, FIRST, 0)
     for copy in gather_b2:
-        copy.start()
-    compute(0, 20, SRC)
-    scatter_a = reduce_out(0)
-    for copy in gather_b2:
-        copy.wait_recv()
-    compute(1, 0, SRC)
-    scatter_b = reduce_out(1)
-
-    for copy in scatter_b:
+        copy.wait_recv()
+    send_out(0, FIRST - 1)
+    compute(1, 0, SRC, 0)
+    scatter_b = scatter_first(1)
+    start(scatter_b)
+    send_out(1, SRC - 1)
+    compute(0, FIRST, FIRST + 6, FIRST)
+    scatter_b2 = scatter_second(1, scatter_b)
+    start(scatter_b2)
+    compute(0, FIRST + 6, FIRST + 12, FIRST)
+    for copy in scatter_b[2:] + scatter_b2:
         copy.wait_recv()
 
     def far(n, carry):
@@ -284,10 +327,16 @@
     back_first = remote(bsend, brelay, bz_send.at[0], bz_recv.at[0], (z_next, x))
     back_second = remote(brelay, bfinal, bz_send.at[1], bz_recv.at[1], (z_next, x))
     back_first.start()
-    for copy in scatter_a:
-        copy.wait_recv()
+    compute(0, FIRST + 12, SRC, FIRST)
+    scatter_a = scatter_first(0)
+    start(scatter_a)
+    send_out(0, SRC - 1)
+    scatter_a2 = scatter_second(0, scatter_a)
+    start(scatter_a2)
     back_first.wait_recv()
     back_second.start()
+    for copy in scatter_a[2:] + scatter_a2:
+        copy.wait_recv()
     back_second.wait_recv()
 
     def near(n, carry):
@@ -320,8 +369,8 @@
         lax.fori_loop(0, SRC, step, 0)
 
     for copy in (
-        shift_first + shift_second + gather_a + gather_a2 + gather_b + gather_b2 + scatter_a + scatter_b
-        + [back_first, back_second]
+        shift_first + shift_second + gather_a + gather_a2 + gather_b + gather_b2 + scatter_a + scatter_a2 + scatter_b
+        + scatter_b2 + [back_first, back_second]
     ):
         copy.wait_send()
     drain(0)
@@ -338,7 +387,9 @@
     item = jnp.arange(flat.shape[0], dtype=jnp.int32)
     src = item // 4
     k = (src // (YS * CS) - z + 1 + c + ZS) % ZS
-    step = ((src % CS - c + CS) % CS) * 16 + (((src // CS) % YS - y + YS) % YS) * 4 + k
+    j = (k + 3 - c) % 4
+    n = ((src % CS - c + CS) % CS) * YS + ((src // CS) % YS - y + YS) % YS
+    step = jnp.where(j == 0, n, 8 + 3 * n + j - 1)
     slot = jnp.where(k < 4, step * 4 + item % 4, -1)
     same = (rows[:, None] == rows[None, :]) & (slot[None, :] < slot[:, None])
     before = jnp.max(jnp.where(same, slot[None, :], -1), axis=1)
@@ -366,15 +417,20 @@
             pltpu.VMEM((STORED, NEIGH_LEN, HEAD_DIM), bf16),
             pltpu.VMEM((ITEMS + 1, HEAD_DIM, NEIGH_LEN), jnp.float32),
             pltpu.VMEM((ITEMS + 1, HEAD_DIM, NEIGH_LEN), jnp.float32),
+            pltpu.VMEM((ITEMS + 1, HEAD_DIM, NEIGH_LEN), jnp.float32),
+            pltpu.VMEM((ITEMS + 1, HEAD_DIM, NEIGH_LEN), jnp.float32),
             pltpu.VMEM((2, XS, 2, ROWS, HEAD_DIM, NEIGH_LEN), bf16),
-            pltpu.VMEM((2, XS - 1, 2, ROWS, HEAD_DIM, NEIGH_LEN), bf16),
+            pltpu.VMEM((2, 2, ROWS, HEAD_DIM, NEIGH_LEN), bf16),
+            pltpu.VMEM((2, 2, ROWS, HEAD_DIM, NEIGH_LEN), bf16),
+            pltpu.VMEM((2, 2, ROWS, HEAD_DIM, NEIGH_LEN), bf16),
+            pltpu.VMEM((2, 2, ROWS, HEAD_DIM, NEIGH_LEN), bf16),
             pltpu.VMEM((2, ROWS, NEIGH_LEN, HEAD_DIM), bf16),
             pltpu.VMEM((2, ROWS, HEAD_DIM, NEIGH_LEN), bf16),
             pltpu.VMEM((2, ROWS, HEAD_DIM, NEIGH_LEN), bf16),
             pltpu.VMEM((2, ROWS, HEAD_DIM, NEIGH_LEN), bf16),
             dma((2, SRC)), dma((2, SRC)), dma((2, SRC)), dma((2, SRC)),
             dma((2,)), dma((2, 3, 2)), dma((2, 3, 2)), dma((2, 2)), dma((2, 2)),
-            dma((2, XS - 1)), dma((2, XS - 1)), dma((2,)), dma((2,)),
+            dma((2, 3, 2)), dma((2, 3, 2)), dma((2,)), dma((2,)),
         ],
         compiler_params=pltpu.CompilerParams(
             collective_id=0, has_side_effects=True, vmem_limit_bytes=60 * 1024 * 1024

time: 213 us -> 175 us (0.82)
  the two profiles are of different devices: /device:TPU:1 before, /device:TPU:54 now
where the time goes in v2:
time: 175 us
  Pallas kernels  166 us (95%)
  local copies, waits for them, and re-layouts  6.5 us (4%)
  other arithmetic  2.2 us (1%)
    pallas_call x1, Pallas kernels, on_device(): pl.pallas_call(kernel, out_shape=(jax.ShapeDtypeStruct((2, TOKENS, querie...  166 us
    slice x1, local copies, waits for them, and re-layouts, on_device(): return (out[0][None], out[1][None], grads[0], grads[1])  4.73 us

profile of v2, /device:TPU:54, one launch (start us, length us, event | category | flops | bytes accessed | tf_op | source)
XLA Modules:
  0.0 175.0 jit_solution(16182305103232416079)
XLA Ops:
  0.7 0.8 copy.11
  1.5 0.1 eq.63
  1.6 0.7 select_reduce_fusion.2.rows_ref
  2.4 0.0 copy-start.1
  2.4 0.1 select_reduce_fusion.1
  2.5 0.2 select_reduce_fusion
  2.7 0.6 compare_select_fusion.prev_ref
  3.3 0.5 compare_select_fusion.1.last_ref
  3.8 0.0 copy-done.1
  3.8 165.6 %retrieval_attention.1 = (bf16[2,128,8192]{2,1,0:T(8,128)(2,1)}, bf16[2,8,128,128]{3,2,1,0:T(8,128)(2,1)}) custom-call(s32[256]{0:T(256)} %copy-done.1, s32[256]{0:T(256)} %compare_select_fusion.prev_ref, s32[32]{0:T(128)} %compare_select_fusion.1.last_ref, bf16[128,8192]{1,0:T(8,128)(2,1)} %bitcast.6, bf16[128,8192]{1,0:T(8,128)(2,1)} %bitcast.7, ...), custom_call_target="tpu_custom_call" | custom-call | tf_op jit(solution)/shard_map/retrieval_attention/pallas_call | solution.py:403
  169.4 0.0 copy-start
  169.4 4.7 %fusion.14 = (bf16[1,128,8192]{2,1,0:T(8,128)(2,1)}, bf16[1,128,8192]{2,1,0:T(8,128)(2,1)}) fusion(bf16[2,128,8192]{2,1,0:T(8,128)(2,1)} %get-tuple-element.6), kind=kLoop, calls=%fused_computation.53 | loop fusion | bytes 8388608 | tf_op jit(solution)/shard_map/slice | solution.py:440
  174.2 0.0 copy-done
  174.2 0.8 slice_bitcast_fusion
  (1 shorter events, 0.0 us)
Async XLA Ops:
  2.4 1.4 copy-start.1
  169.4 4.7 %copy-start = (bf16[2,8,128,128]{3,2,1,0:T(8,128)(2,1)S(1)}, bf16[2,8,128,128]{3,2,1,0:T(8,128)(2,1)}, u32[]{:S(2)}) copy-start(bf16[2,8,128,128]{3,2,1,0:T(8,128)(2,1)} %get-tuple-element.7) | copy-start | bytes 1572868

commit v3 on v2

v3 whole, which is shorter than its diff:
```python
import functools
import math

import jax
import jax.numpy as jnp
from jax import lax
from jax.experimental import pallas as pl
from jax.experimental.pallas import tpu as pltpu
from jax.sharding import PartitionSpec as P

HEAD_DIM = 128
GROUP = 64
NEIGH_LEN = 128
MESH = pl.DeviceIdType.MESH
ZS, YS, CS, XS = 8, 4, 2, 4
TOKENS = 128
ROWS = 8
STORED = ROWS * XS
PEERS = YS * CS
NEAR, MID, FAR = range(3)
OFFSETS = ((0, -1, -2), (0, -1, 1), (0, 1))
BASE = (0, 24, 48)
STEPS = 64
ZERO = STEPS * 4


def kernel(
    rows_ref, prev_ref, last_ref, q_ref, g_ref, ck_ref, cv_ref,
    out_ref, grad_ref,
    rbuf, obuf, ka, va, km, vm, kf, vf, tk, tv, dsend, dfar, dnear, dring, bsend, bmid, msend, bfinal,
    in_send, in_recv, out_send, out_recv, own_sem, ag_send, ag_recv, zs_send, zs_recv, rs_send, rs_recv, bz_send, bz_recv,
):
    scale = 1.0 / math.sqrt(HEAD_DIM)
    seq = lax.axis_index("seq")
    x = lax.axis_index("grp")
    z, y, c = seq // (YS * CS), (seq // CS) % YS, seq % CS
    right, left = (x + 1) % XS, (x + XS - 1) % XS

    def at(zz, yy, cc):
        return (zz * YS + yy) * CS + cc

    sign = 1 - 2 * c
    z_next, z_back = at((z + 2 * sign + ZS) % ZS, y, c), at((z - 2 * sign + ZS) % ZS, y, c)

    def source(e, n):
        return at((z + e * sign + ZS) % ZS, (y + n % YS) % YS, (c + n // YS) % CS)

    def dest(e, n):
        cc = (c + n // YS) % CS
        return at((z - e * (1 - 2 * cc) + ZS) % ZS, (y - n % YS + YS) % YS, cc)

    def head_of(device, which):
        if which == MID:
            return (device - 2 * (1 - 2 * (device % CS)) * PEERS + ZS * PEERS) % (ZS * PEERS)
        return (device + (which == FAR) * (ZS // 2) * PEERS) % (ZS * PEERS)

    def slot_of(which, e):
        return BASE[which] + OFFSETS[which].index(e) * PEERS

    def columns(head):
        return pl.ds(pl.multiple_of(head * HEAD_DIM, HEAD_DIM), HEAD_DIM)

    barrier = pltpu.get_barrier_semaphore()

    def greet(n, carry):
        zz = (z + ZS - 2 + n // (YS * CS)) % ZS
        peer = at(zz, (n // CS) % YS, n % CS)

        @pl.when(peer != seq)
        def _():
            pl.semaphore_signal(barrier, inc=1, device_id=(peer, x), device_id_type=MESH)

        return carry

    lax.fori_loop(0, 5 * YS * CS, greet, 0)
    for o in range(1, XS):
        pl.semaphore_signal(barrier, inc=1, device_id=(seq, (x + o) % XS), device_id_type=MESH)
    pl.semaphore_wait(barrier, 5 * YS * CS - 1 + XS - 1)

    def remote(src, dst, send, recv, device):
        return pltpu.make_async_remote_copy(
            src_ref=src, dst_ref=dst, send_sem=send, recv_sem=recv, device_id=device, device_id_type=MESH
        )

    def block(owner):
        return pl.ds(pl.multiple_of(owner * ROWS, ROWS), ROWS)

    mine = block(x)
    caches = ((ka, va), (km, vm), (kf, vf))

    def gather_first(which, srcs):
        copies = []
        for kv in range(2):
            dst = caches[which][kv].at[mine]
            copies.append(remote(srcs[kv], dst, ag_send.at[which, 0, kv], ag_recv.at[which, 0, kv], (seq, right)))
            copies.append(remote(srcs[kv], dst, ag_send.at[which, 1, kv], ag_recv.at[which, 1, kv], (seq, left)))
        return copies

    def gather_second(which):
        near = caches[which]
        from_left, from_right = near[0].at[block(left)], near[1].at[block(right)]
        return [
            remote(from_left, from_left, ag_send.at[which, 2, 0], ag_recv.at[which, 2, 0], (seq, right)),
            remote(from_right, from_right, ag_send.at[which, 2, 1], ag_recv.at[which, 2, 1], (seq, left)),
        ]

    own = [
        pltpu.make_async_copy(ck_ref, ka.at[mine], own_sem.at[0]),
        pltpu.make_async_copy(cv_ref, va.at[mine], own_sem.at[1]),
    ]
    def start(copies):
        for copy in copies:
            copy.start()

    def arrive(copies):
        for copy in copies:
            copy.wait_recv()

    gather_a = gather_first(NEAR, (ck_ref, cv_ref))
    shift_first = [
        remote(src, caches[MID][kv].at[mine], zs_send.at[0, kv], zs_recv.at[0, kv], (z_next, x))
        for kv, src in enumerate((ck_ref, cv_ref))
    ]
    shift_second = [
        remote(caches[MID][kv].at[mine], caches[FAR][kv].at[mine], zs_send.at[1, kv], zs_recv.at[1, kv], (z_next, x))
        for kv in range(2)
    ]
    start(shift_first + gather_a + own)

    def in_copies(which, e, n):
        device = dest(e, n)
        cols = columns(head_of(device, which))
        i = slot_of(which, e) + n
        return [
            (src.at[:, cols], rbuf.at[i, m], in_send.at[i], in_recv.at[i], (device, x))
            for m, src in enumerate((q_ref, g_ref))
        ]

    def send_in(which, e):
        def step(n, carry):
            here = dest(e, n) == seq

            @pl.when(here)
            def _():
                for src, dst, _send, recv, _device in in_copies(which, e, n):
                    pltpu.make_async_copy(src, dst, recv).start()

            @pl.when(jnp.logical_not(here))
            def _():
                for args in in_copies(which, e, n):
                    remote(*args).start()

            return carry

        lax.fori_loop(0, PEERS, step, 0)

    send_in(NEAR, 0)
    send_in(MID, 0)
    for kv in range(2):
        shift_first[kv].wait_recv()
        shift_second[kv].start()
    gather_m = gather_first(MID, (km.at[mine], vm.at[mine]))
    start(gather_m)
    send_in(NEAR, -1)
    gather_a2 = gather_second(NEAR)
    arrive(gather_a)
    start(gather_a2)
    for which, e in ((FAR, 0), (FAR, 1), (MID, -1), (MID, 1), (NEAR, -2)):
        send_in(which, e)

    for ref in (tk, tv):
        ref[ZERO] = jnp.zeros((HEAD_DIM, NEIGH_LEN), jnp.float32)
    for copy in own:
        copy.wait()
    arrive(gather_a2)

    def nt(a, b):
        return lax.dot_general(a, b, (((1,), (1,)), ((), ())), preferred_element_type=jnp.float32)

    def nn(a, b):
        return lax.dot_general(a, b, (((1,), (0,)), ((), ())), preferred_element_type=jnp.float32)

    def tn(a, b):
        return lax.dot_general(a, b, (((0,), (0,)), ((), ())), preferred_element_type=jnp.float32)

    def attend(which, e, n):
        kref, vref = caches[which]
        first = source(e, n) * 4
        i = slot_of(which, e) + n
        chain = which * rows_ref.shape[0] + first
        both = range(2)
        spans = [pl.ds(g * GROUP, GROUP) for g in both]
        qs = [rbuf[i, 0, span, :] for span in spans]
        cts = [rbuf[i, 1, span, :] for span in spans]
        near = [[rows_ref[first + 2 * g + j] for j in range(2)] for g in both]
        keys = [jnp.concatenate([kref[r] for r in near[g]], axis=0) for g in both]
        vals = [jnp.concatenate([vref[r] for r in near[g]], axis=0) for g in both]
        raw = [nt(qs[g], keys[g]) for g in both]
        pg = [nt(cts[g], vals[g]) for g in both]
        tops = [jnp.max(raw[g], axis=-1, keepdims=True) for g in both]
        weights = [jnp.exp((raw[g] - tops[g]) * scale) for g in both]
        sums = [jnp.sum(weights[g], axis=-1, keepdims=True) for g in both]
        crossed = [jnp.sum(weights[g] * pg[g], axis=-1, keepdims=True) for g in both]
        shares = [1.0 / sums[g] for g in both]
        prob = [weights[g] * shares[g] for g in both]
        low = [prob[g].astype(jnp.bfloat16) for g in both]
        sg = [(prob[g] * ((pg[g] - crossed[g] * shares[g]) * scale)).astype(jnp.bfloat16) for g in both]
        attended = [nn(low[g], vals[g]) for g in both]
        grads = [nn(sg[g], keys[g]) for g in both]
        vt = [tn(cts[g], low[g]) for g in both]
        kt = [tn(qs[g], sg[g]) for g in both]
        for g in both:
            obuf[i, 0, spans[g], :] = attended[g].astype(jnp.bfloat16)
            obuf[i, 1, spans[g], :] = grads[g].astype(jnp.bfloat16)
        for g in both:
            for j in range(2):
                before = prev_ref[chain + 2 * g + j]
                lanes = slice(j * NEIGH_LEN, (j + 1) * NEIGH_LEN)
                tk[i * 4 + 2 * g + j] = tk[before] + kt[g][:, lanes]
                tv[i * 4 + 2 * g + j] = tv[before] + vt[g][:, lanes]

    def send_out(which, e, n):
        device = source(e, n)
        cols = columns(head_of(seq, which))
        i = slot_of(which, e) + n
        here = device == seq

        @pl.when(here)
        def _():
            pltpu.make_async_copy(obuf.at[i], out_ref.at[:, :, cols], out_recv.at[i]).start()

        @pl.when(jnp.logical_not(here))
        def _():
            remote(obuf.at[i], out_ref.at[:, :, cols], out_send.at[i], out_recv.at[i], (device, x)).start()

    def compute(which, e, begin=0, end=PEERS, held=None):
        def step(n, carry):
            i = slot_of(which, e) + n
            pltpu.make_async_copy(obuf.at[i], rbuf.at[i], in_recv.at[i]).wait()
            attend(which, e, n)

            @pl.when(n > 0)
            def _():
                send_out(which, e, n - 1)

            if held is not None:

                @pl.when(n == 0)
                def _():
                    send_out(held[0], held[1], PEERS - 1)

            return carry

        lax.fori_loop(begin, end, step, 0)

    def add(refs):
        total = refs[0][...].astype(jnp.float32)
        for ref in refs[1:]:
            total = total + ref[...].astype(jnp.float32)
        return total

    far_owner = (x + 2) % XS
    toward, away = (right, left), (left, right)

    def scatter_first(which):
        def step(r, carry):
            slot = last_ref[which * STORED + r]
            dsend[which, r // ROWS, 0, r % ROWS] = tk[slot].astype(jnp.bfloat16)
            dsend[which, r // ROWS, 1, r % ROWS] = tv[slot].astype(jnp.bfloat16)
            return carry

        lax.fori_loop(0, STORED, step, 0)
        copies = []
        for kv in range(2):
            copies.append(
                remote(
                    dsend.at[which, far_owner, kv], dfar.at[which, kv], rs_send.at[which, 0, kv], rs_recv.at[which, 0, kv],
                    (seq, toward[kv]),
                )
            )
        for kv in range(2):
            copies.append(
                remote(
                    dsend.at[which, away[kv], kv], dnear.at[which, kv], rs_send.at[which, 1, kv], rs_recv.at[which, 1, kv],
                    (seq, away[kv]),
                )
            )
        return copies

    def scatter_second(which, first_copies):
        copies = []
        for kv in range(2):
            first_copies[kv].wait_recv()

            def step(r, carry, kv=kv):
                mine_ref = dsend.at[which, toward[kv], kv, r]
                mine_ref[...] = add((mine_ref, dfar.at[which, kv, r])).astype(jnp.bfloat16)
                return carry

            lax.fori_loop(0, ROWS, step, 0)
            copies.append(
                remote(
                    dsend.at[which, toward[kv], kv], dring.at[which, kv], rs_send.at[which, 2, kv], rs_recv.at[which, 2, kv],
                    (seq, toward[kv]),
                )
            )
        return copies

    def summed(which, kv, r):
        return add((dsend.at[which, x, kv, r], dnear.at[which, kv, r], dring.at[which, kv, r]))

    compute(NEAR, 0)
    gather_m2 = gather_second(MID)
    arrive(gather_m)
    start(gather_m2)
    arrive(shift_second)
    gather_f = gather_first(FAR, (kf.at[mine], vf.at[mine]))
    start(gather_f)
    compute(NEAR, -1, held=(NEAR, 0))
    arrive(gather_m2)
    gather_f2 = gather_second(FAR)
    compute(MID, 0, held=(NEAR, -1))
    arrive(gather_f)
    start(gather_f2)
    arrive(gather_f2)
    compute(FAR, 0, held=(MID, 0))
    compute(FAR, 1, held=(FAR, 0))
    scatter_f = scatter_first(FAR)
    start(scatter_f)
    compute(MID, -1, held=(FAR, 1))
    scatter_f2 = scatter_second(FAR, scatter_f)
    start(scatter_f2)
    compute(MID, 1, held=(MID, -1))
    scatter_m = scatter_first(MID)
    start(scatter_m)
    arrive(scatter_f[2:] + scatter_f2)

    def far(n, carry):
        kv, r = n // ROWS, n % ROWS
        bsend[kv, r] = summed(FAR, kv, r).astype(jnp.bfloat16)
        return carry

    lax.fori_loop(0, 2 * ROWS, far, 0)
    back_first = remote(bsend, bmid, bz_send.at[0], bz_recv.at[0], (z_back, x))
    back_second = remote(msend, bfinal, bz_send.at[1], bz_recv.at[1], (z_back, x))
    back_first.start()
    compute(NEAR, -2, held=(MID, 1))
    scatter_m2 = scatter_second(MID, scatter_m)
    start(scatter_m2)
    scatter_a = scatter_first(NEAR)
    start(scatter_a)
    send_out(NEAR, -2, PEERS - 1)
    arrive(scatter_m[2:] + scatter_m2)
    back_first.wait_recv()

    def middle(n, carry):
        kv, r = n // ROWS, n % ROWS
        msend[kv, r] = (summed(MID, kv, r) + bmid[kv, r].astype(jnp.float32)).astype(jnp.bfloat16)
        return carry

    lax.fori_loop(0, 2 * ROWS, middle, 0)
    back_second.start()
    scatter_a2 = scatter_second(NEAR, scatter_a)
    start(scatter_a2)
    arrive(scatter_a[2:] + scatter_a2)
    back_second.wait_recv()

    def near(n, carry):
        kv, r = n // ROWS, n % ROWS
        total = summed(NEAR, kv, r) + bfinal[kv, r].astype(jnp.float32)
        grad_ref[kv, r] = total.T.astype(jnp.bfloat16)
        return carry

    lax.fori_loop(0, 2 * ROWS, near, 0)

    def drain(which, e):
        def step(n, carry):
            i = slot_of(which, e) + n
            pltpu.make_async_copy(obuf.at[i], out_ref.at[:, :, columns(0)], out_recv.at[i]).wait()

            @pl.when(dest(e, n) != seq)
            def _():
                remote(obuf.at[i], rbuf.at[i], in_send.at[i], in_recv.at[i], (dest(e, n), x)).wait_send()

            @pl.when(source(e, n) != seq)
            def _():
                remote(
                    obuf.at[i], out_ref.at[:, :, columns(0)], out_send.at[i], out_recv.at[i], (source(e, n), x)
                ).wait_send()

            return carry

        lax.fori_loop(0, PEERS, step, 0)

    for copy in (
        shift_first + shift_second + gather_a + gather_a2 + gather_m + gather_m2 + gather_f + gather_f2 + scatter_a
        + scatter_a2 + scatter_m + scatter_m2 + scatter_f + scatter_f2 + [back_first, back_second]
    ):
        copy.wait_send()
    for which in (NEAR, MID, FAR):
        for e in OFFSETS[which]:
            drain(which, e)


def on_device(queries, cotangent, cache_keys, cache_values, block_table, block_slot):
    seq = lax.axis_index("seq")
    z, y, c = seq // (YS * CS), (seq // CS) % YS, seq % CS
    flat = block_table[0].reshape(-1)
    blocks = block_slot.shape[0]
    hit = flat[:, None] == jnp.arange(blocks, dtype=jnp.int32)[None, :]
    rows = jnp.sum(jnp.where(hit, block_slot[None, :], 0), axis=1)
    item = jnp.arange(flat.shape[0], dtype=jnp.int32)
    src = item // 4
    away = ((src // PEERS - z) * (1 - 2 * c) + ZS) % ZS
    n = ((src % CS - c + CS) % CS) * YS + ((src // CS) % YS - y + YS) % YS
    slots = []
    for which in (NEAR, MID, FAR):
        slot = jnp.full_like(item, -1)
        for b, e in enumerate(OFFSETS[which]):
            slot = jnp.where(away == e % ZS, (BASE[which] + b * PEERS + n) * 4 + item % 4, slot)
        slots.append(slot)
    slot = jnp.stack(slots)
    same = (rows[:, None] == rows[None, :])[None] & (slot[:, None, :] < slot[:, :, None])
    before = jnp.max(jnp.where(same, slot[:, None, :], -1), axis=2)
    before = jnp.where(before < 0, ZERO, before).reshape(-1)
    owned = (rows[None, :] == jnp.arange(STORED, dtype=jnp.int32)[:, None])[None]
    final = jnp.max(jnp.where(owned, slot[:, None, :], -1), axis=2)
    final = jnp.where(final < 0, ZERO, final).reshape(-1)
    smem = pl.BlockSpec(memory_space=pltpu.SMEM)
    hbm = pl.BlockSpec(memory_space=pl.ANY)
    bf16 = jnp.bfloat16
    dma = pltpu.SemaphoreType.DMA
    out, grads = pl.pallas_call(
        kernel,
        out_shape=(
            jax.ShapeDtypeStruct((2, TOKENS, queries.shape[2]), bf16),
            jax.ShapeDtypeStruct((2, ROWS, NEIGH_LEN, HEAD_DIM), bf16),
        ),
        in_specs=[smem, smem, smem, hbm, hbm, hbm, hbm],
        out_specs=(hbm, pl.BlockSpec(memory_space=pltpu.VMEM)),
        scratch_shapes=[
            pltpu.VMEM((STEPS, 2, TOKENS, HEAD_DIM), bf16),
            pltpu.VMEM((STEPS, 2, TOKENS, HEAD_DIM), bf16),
            *[pltpu.VMEM((STORED, NEIGH_LEN, HEAD_DIM), bf16)] * 6,
            *[pltpu.VMEM((ZERO + 1, HEAD_DIM, NEIGH_LEN), jnp.float32)] * 2,
            pltpu.VMEM((3, XS, 2, ROWS, HEAD_DIM, NEIGH_LEN), bf16),
            *[pltpu.VMEM((3, 2, ROWS, HEAD_DIM, NEIGH_LEN), bf16)] * 3,
            *[pltpu.VMEM((2, ROWS, HEAD_DIM, NEIGH_LEN), bf16)] * 4,
            dma((STEPS,)), dma((STEPS,)), dma((STEPS,)), dma((STEPS,)),
            dma((2,)), dma((3, 3, 2)), dma((3, 3, 2)), dma((2, 2)), dma((2, 2)),
            dma((3, 3, 2)), dma((3, 3, 2)), dma((2,)), dma((2,)),
        ],
        compiler_params=pltpu.CompilerParams(
            collective_id=0, has_side_effects=True, vmem_limit_bytes=67043328
        ),
        name="retrieval_attention",
    )(rows, before, final, queries[0], cotangent[0], cache_keys, cache_values)
    return out[0][None], out[1][None], grads[0], grads[1]


def solution(mesh):
    placed = (
        P("grp", "seq", None),
        P("grp", "seq", None),
        P("grp", None, "seq"),
        P("grp", None, "seq"),
        P("grp", None, None),
        P(),
    )
    return jax.shard_map(
        on_device,
        mesh=mesh,
        in_specs=placed,
        out_specs=(
            P("grp", "seq", None),
            P("grp", "seq", None),
            P("grp", None, "seq"),
            P("grp", None, "seq"),
        ),
        check_vma=False,
    )
```

time: 175 us -> 153 us (0.87)
  the two profiles are of different devices: /device:TPU:54 before, /device:TPU:1 now
where the time goes in v3:
time: 153 us; the launch traced here: 151 us
  Pallas kernels  141 us (92%)
  local copies, waits for them, and re-layouts  6.59 us (4%)
  other arithmetic  2.57 us (2%)
    pallas_call x1, Pallas kernels, on_device(): pl.pallas_call(kernel, out_shape=(jax.ShapeDtypeStruct((2, TOKENS, querie...  141 us
    slice x1, local copies, waits for them, and re-layouts, on_device(): return (out[0][None], out[1][None], grads[0], grads[1])  4.73 us

profile of v3, /device:TPU:1, one launch (start us, length us, event | category | flops | bytes accessed | tf_op | source)
XLA Modules:
  0.0 151.0 jit_solution(12347115882820431343)
XLA Ops:
  0.8 0.8 copy.11
  1.6 0.1 eq.129
  1.7 0.7 select_reduce_fusion.2.rows_ref
  2.5 0.0 copy-start.1
  2.5 0.1 select_reduce_fusion.1
  2.6 0.1 reduce_max.25
  2.7 0.5 compare_select_fusion.10.last_ref
  3.2 0.1 broadcast_compare_fusion
  3.3 0.4 select_reduce_fusion
  3.7 0.0 copy-done.1
  3.7 0.6 compare_select_fusion.prev_ref
  4.3 141.1 %retrieval_attention.1 = (bf16[2,128,8192]{2,1,0:T(8,128)(2,1)}, bf16[2,8,128,128]{3,2,1,0:T(8,128)(2,1)}) custom-call(s32[256]{0:T(256)} %copy-done.1, s32[768]{0:T(1024)} %compare_select_fusion.prev_ref, s32[96]{0:T(128)} %compare_select_fusion.10.last_ref, bf16[128,8192]{1,0:T(8,128)(2,1)} %bitcast.6, bf16[128,8192]{1,0:T(8,128)(2,1)} %bitcast.7, ...), custom_call_target="tpu_custom_call" | custom-call | tf_op jit(solution)/shard_map/retrieval_attention/pallas_call | solution.py:433
  145.4 0.0 copy-start
  145.5 4.7 %fusion.10 = (bf16[1,128,8192]{2,1,0:T(8,128)(2,1)}, bf16[1,128,8192]{2,1,0:T(8,128)(2,1)}) fusion(bf16[2,128,8192]{2,1,0:T(8,128)(2,1)} %get-tuple-element.6), kind=kLoop, calls=%fused_computation.52 | loop fusion | bytes 8388608 | tf_op jit(solution)/shard_map/slice | solution.py:458
  150.2 0.0 copy-done
  150.2 0.8 slice_bitcast_fusion
  (5 shorter events, 0.1 us)
Async XLA Ops:
  2.5 1.2 copy-start.1
  145.4 4.7 %copy-start = (bf16[2,8,128,128]{3,2,1,0:T(8,128)(2,1)S(1)}, bf16[2,8,128,128]{3,2,1,0:T(8,128)(2,1)}, u32[]{:S(2)}) copy-start(bf16[2,8,128,128]{3,2,1,0:T(8,128)(2,1)} %get-tuple-element.7) | copy-start | bytes 1572868

commit v4 on v3

--- a/solution.py
+++ b/solution.py
@@ -138,21 +138,14 @@
 
     def send_in(which, e):
         def step(n, carry):
-            here = dest(e, n) == seq
-
-            @pl.when(here)
-            def _():
-                for src, dst, _send, recv, _device in in_copies(which, e, n):
-                    pltpu.make_async_copy(src, dst, recv).start()
-
-            @pl.when(jnp.logical_not(here))
-            def _():
-                for args in in_copies(which, e, n):
-                    remote(*args).start()
-
+            for args in in_copies(which, e, n):
+                remote(*args).start()
             return carry
 
-        lax.fori_loop(0, PEERS, step, 0)
+        if e == 0:
+            for src, dst, _send, recv, _device in in_copies(which, e, 0):
+                pltpu.make_async_copy(src, dst, recv).start()
+        lax.fori_loop(1 if e == 0 else 0, PEERS, step, 0)
 
     send_in(NEAR, 0)
     send_in(MID, 0)
@@ -165,7 +158,7 @@
     gather_a2 = gather_second(NEAR)
     arrive(gather_a)
     start(gather_a2)
-    for which, e in ((FAR, 0), (FAR, 1), (MID, -1), (MID, 1), (NEAR, -2)):
+    for which, e in ((MID, -1), (FAR, 0), (FAR, 1), (MID, 1), (NEAR, -2)):
         send_in(which, e)
 
     for ref in (tk, tv):
@@ -223,15 +216,18 @@
         device = source(e, n)
         cols = columns(head_of(seq, which))
         i = slot_of(which, e) + n
-        here = device == seq
-
-        @pl.when(here)
+
+        def away():
+            remote(obuf.at[i], out_ref.at[:, :, cols], out_send.at[i], out_recv.at[i], (device, x)).start()
+
+        if e != 0:
+            away()
+            return
+        pl.when(n > 0)(away)
+
+        @pl.when(n == 0)
         def _():
             pltpu.make_async_copy(obuf.at[i], out_ref.at[:, :, cols], out_recv.at[i]).start()
-
-        @pl.when(jnp.logical_not(here))
-        def _():
-            remote(obuf.at[i], out_ref.at[:, :, cols], out_send.at[i], out_recv.at[i], (device, x)).start()
 
     def compute(which, e, begin=0, end=PEERS, held=None):
         def step(n, carry):
@@ -318,21 +314,23 @@
     start(gather_f)
     compute(NEAR, -1, held=(NEAR, 0))
     arrive(gather_m2)
+    compute(MID, 0, held=(NEAR, -1))
     gather_f2 = gather_second(FAR)
-    compute(MID, 0, held=(NEAR, -1))
     arrive(gather_f)
     start(gather_f2)
+    compute(MID, -1, held=(MID, 0))
     arrive(gather_f2)
-    compute(FAR, 0, held=(MID, 0))
+    compute(FAR, 0, held=(MID, -1))
     compute(FAR, 1, held=(FAR, 0))
     scatter_f = scatter_first(FAR)
     start(scatter_f)
-    compute(MID, -1, held=(FAR, 1))
+    compute(MID, 1, 0, 6, held=(FAR, 1))
     scatter_f2 = scatter_second(FAR, scatter_f)
     start(scatter_f2)
-    compute(MID, 1, held=(MID, -1))
+    compute(MID, 1, 6, PEERS)
     scatter_m = scatter_first(MID)
     start(scatter_m)
+    compute(NEAR, -2, 0, 4, held=(MID, 1))
     arrive(scatter_f[2:] + scatter_f2)
 
     def far(n, carry):
@@ -344,9 +342,10 @@
     back_first = remote(bsend, bmid, bz_send.at[0], bz_recv.at[0], (z_back, x))
     back_second = remote(msend, bfinal, bz_send.at[1], bz_recv.at[1], (z_back, x))
     back_first.start()
-    compute(NEAR, -2, held=(MID, 1))
+    compute(NEAR, -2, 4, 6)
     scatter_m2 = scatter_second(MID, scatter_m)
     start(scatter_m2)
+    compute(NEAR, -2, 6, PEERS)
     scatter_a = scatter_first(NEAR)
     start(scatter_a)
     send_out(NEAR, -2, PEERS - 1)
@@ -362,7 +361,27 @@
     back_second.start()
     scatter_a2 = scatter_second(NEAR, scatter_a)
     start(scatter_a2)
+
+    def drain(which, e):
+        def sent(n, carry):
+            i = slot_of(which, e) + n
+            pltpu.make_async_copy(obuf.at[i], rbuf.at[i], in_send.at[i]).wait()
+            pltpu.make_async_copy(obuf.at[i], rbuf.at[i], out_send.at[i]).wait()
+            return carry
+
+        def came(n, carry):
+            i = slot_of(which, e) + n
+            pltpu.make_async_copy(obuf.at[i], rbuf.at[i], out_recv.at[i]).wait()
+            return carry
+
+        lax.fori_loop(1 if e == 0 else 0, PEERS, sent, 0)
+        lax.fori_loop(0, PEERS, came, 0)
+
+    drain(NEAR, 0)
+    drain(NEAR, -1)
     arrive(scatter_a[2:] + scatter_a2)
+    for which, e in ((MID, 0), (MID, -1), (FAR, 0), (FAR, 1)):
+        drain(which, e)
     back_second.wait_recv()
 
     def near(n, carry):
@@ -373,33 +392,32 @@
 
     lax.fori_loop(0, 2 * ROWS, near, 0)
 
-    def drain(which, e):
-        def step(n, carry):
-            i = slot_of(which, e) + n
-            pltpu.make_async_copy(obuf.at[i], out_ref.at[:, :, columns(0)], out_recv.at[i]).wait()
-
-            @pl.when(dest(e, n) != seq)
-            def _():
-                remote(obuf.at[i], rbuf.at[i], in_send.at[i], in_recv.at[i], (dest(e, n), x)).wait_send()
-
-            @pl.when(source(e, n) != seq)
-            def _():
-                remote(
-                    obuf.at[i], out_ref.at[:, :, columns(0)], out_send.at[i], out_recv.at[i], (source(e, n), x)
-                ).wait_send()
-
-            return carry
-
-        lax.fori_loop(0, PEERS, step, 0)
-
     for copy in (
         shift_first + shift_second + gather_a + gather_a2 + gather_m + gather_m2 + gather_f + gather_f2 + scatter_a
         + scatter_a2 + scatter_m + scatter_m2 + scatter_f + scatter_f2 + [back_first, back_second]
     ):
         copy.wait_send()
-    for which in (NEAR, MID, FAR):
-        for e in OFFSETS[which]:
-            drain(which, e)
+    drain(MID, 1)
+    drain(NEAR, -2)
+
+
+def settle(out_ref, grad_ref, attended_ref, query_ref, keys_ref, values_ref, rows, blocks, in_sem, out_sem):
+    moves = []
+    for m, dst in enumerate((attended_ref, query_ref)):
+        for r in range(4):
+            span = pl.ds(r * 32, 32)
+            moves.append((out_ref.at[m, span], rows.at[m, span], dst.at[span]))
+    for m, dst in enumerate((keys_ref, values_ref)):
+        moves.append((grad_ref.at[m], blocks.at[m], dst))
+    arriving = [pltpu.make_async_copy(src, mid, in_sem.at[n]) for n, (src, mid, _dst) in enumerate(moves)]
+    leaving = [pltpu.make_async_copy(mid, dst, out_sem.at[n]) for n, (_src, mid, dst) in enumerate(moves)]
+    for copy in arriving:
+        copy.start()
+    for first, second in zip(arriving, leaving):
+        first.wait()
+        second.start()
+    for copy in leaving:
+        copy.wait()
 
 
 def on_device(queries, cotangent, cache_keys, cache_values, block_table, block_slot):
@@ -455,7 +473,21 @@
         ),
         name="retrieval_attention",
     )(rows, before, final, queries[0], cotangent[0], cache_keys, cache_values)
-    return out[0][None], out[1][None], grads[0], grads[1]
+    attended, query_grad, keys_grad, values_grad = pl.pallas_call(
+        settle,
+        out_shape=(
+            jax.ShapeDtypeStruct(out.shape[1:], bf16),
+            jax.ShapeDtypeStruct(out.shape[1:], bf16),
+            jax.ShapeDtypeStruct(grads.shape[1:], bf16),
+            jax.ShapeDtypeStruct(grads.shape[1:], bf16),
+        ),
+        in_specs=[hbm, hbm],
+        out_specs=(hbm,) * 4,
+        scratch_shapes=[pltpu.VMEM(out.shape, bf16), pltpu.VMEM(grads.shape, bf16), dma((10,)), dma((10,))],
+        compiler_params=pltpu.CompilerParams(vmem_limit_bytes=67043328),
+        name="settle",
+    )(out, grads)
+    return attended[None], query_grad[None], keys_grad, values_grad
 
 
 def solution(mesh):

time: 153 us -> 148 us (0.967); the launches traced: 151 us -> 148 us
  local copies, waits for them, and re-layouts: 6.59 us -> 1.02 us
  Pallas kernels: 141 us -> 144 us
    slice x1 -> x0, local copies, waits for them, and re-layouts: 4.73 us -> none  [on_device(): return (out[0][None], out[1][None], grads[0], grads[1])]
    pallas_call x0 -> x1, Pallas kernels: none -> 4.07 us  [on_device(): pl.pallas_call(settle, out_shape=(jax.ShapeDtypeStruct(out.shape[1:], bf1...]
where the time goes in v4:
time: 148 us
  Pallas kernels  144 us (97%)
  other arithmetic  2.57 us (2%)
    pallas_call x1, Pallas kernels, on_device(): pl.pallas_call(kernel, out_shape=(jax.ShapeDtypeStruct((2, TOKENS, querie...  140 us
    pallas_call x1, Pallas kernels, on_device(): pl.pallas_call(settle, out_shape=(jax.ShapeDtypeStruct(out.shape[1:], bf1...  4.07 us

profile of v4, /device:TPU:1, one launch (start us, length us, event | category | flops | bytes accessed | tf_op | source)
XLA Modules:
  0.0 148.2 jit_solution(116094918655298438)
XLA Ops:
  0.8 0.8 copy.11
  1.6 0.1 eq.129
  1.7 0.7 select_reduce_fusion.2.rows_ref
  2.5 0.0 copy-start
  2.5 0.1 select_reduce_fusion.1
  2.6 0.1 reduce_max.25
  2.7 0.5 compare_select_fusion.10.last_ref
  3.2 0.1 broadcast_compare_fusion
  3.3 0.4 select_reduce_fusion
  3.7 0.0 copy-done
  3.7 0.6 compare_select_fusion.prev_ref
  4.3 139.8 %retrieval_attention.1 = (bf16[2,128,8192]{2,1,0:T(8,128)(2,1)}, bf16[2,8,128,128]{3,2,1,0:T(8,128)(2,1)}) custom-call(s32[256]{0:T(256)} %copy-done, s32[768]{0:T(1024)} %compare_select_fusion.prev_ref, s32[96]{0:T(128)} %compare_select_fusion.10.last_ref, bf16[128,8192]{1,0:T(8,128)(2,1)} %bitcast.4, bf16[128,8192]{1,0:T(8,128)(2,1)} %bitcast.5, ...), custom_call_target="tpu_custom_call" | custom-call | tf_op jit(solution)/shard_map/retrieval_attention/pallas_call | solution.py:451
  144.1 4.1 %settle.1 = (bf16[128,8192]{1,0:T(8,128)(2,1)}, bf16[128,8192]{1,0:T(8,128)(2,1)}, bf16[8,128,128]{2,1,0:T(8,128)(2,1)}, bf16[8,128,128]{2,1,0:T(8,128)(2,1)}) custom-call(bf16[2,128,8192]{2,1,0:T(8,128)(2,1)} %get-tuple-element.10.out_ref, bf16[2,8,128,128]{3,2,1,0:T(8,128)(2,1)} %get-tuple-element.11.grad_ref), custom_call_target="tpu_custom_call" | custom-call | tf_op jit(solution)/shard_map/settle/pallas_call | solution.py:476
  (5 shorter events, 0.1 us)
Async XLA Ops:
  2.5 1.2 copy-start

commit v5 on v4

--- a/solution.py
+++ b/solution.py
@@ -176,16 +176,15 @@
     def tn(a, b):
         return lax.dot_general(a, b, (((0,), (0,)), ((), ())), preferred_element_type=jnp.float32)
 
-    def attend(which, e, n):
+    def attend(which, e, steps):
         kref, vref = caches[which]
-        first = source(e, n) * 4
-        i = slot_of(which, e) + n
-        chain = which * rows_ref.shape[0] + first
-        both = range(2)
-        spans = [pl.ds(g * GROUP, GROUP) for g in both]
-        qs = [rbuf[i, 0, span, :] for span in spans]
-        cts = [rbuf[i, 1, span, :] for span in spans]
-        near = [[rows_ref[first + 2 * g + j] for j in range(2)] for g in both]
+        firsts = [source(e, n) * 4 for n in steps]
+        slots = [slot_of(which, e) + n for n in steps]
+        both = range(2 * len(steps))
+        at_slot = [(slots[g // 2], pl.ds(g % 2 * GROUP, GROUP)) for g in both]
+        qs = [rbuf[i, 0, span, :] for i, span in at_slot]
+        cts = [rbuf[i, 1, span, :] for i, span in at_slot]
+        near = [[rows_ref[firsts[g // 2] + g % 2 * 2 + j] for j in range(2)] for g in both]
         keys = [jnp.concatenate([kref[r] for r in near[g]], axis=0) for g in both]
         vals = [jnp.concatenate([vref[r] for r in near[g]], axis=0) for g in both]
         raw = [nt(qs[g], keys[g]) for g in both]
@@ -202,15 +201,15 @@
         grads = [nn(sg[g], keys[g]) for g in both]
         vt = [tn(cts[g], low[g]) for g in both]
         kt = [tn(qs[g], sg[g]) for g in both]
-        for g in both:
-            obuf[i, 0, spans[g], :] = attended[g].astype(jnp.bfloat16)
-            obuf[i, 1, spans[g], :] = grads[g].astype(jnp.bfloat16)
-        for g in both:
+        for g, (i, span) in enumerate(at_slot):
+            obuf[i, 0, span, :] = attended[g].astype(jnp.bfloat16)
+            obuf[i, 1, span, :] = grads[g].astype(jnp.bfloat16)
+        for g, (i, _span) in enumerate(at_slot):
             for j in range(2):
-                before = prev_ref[chain + 2 * g + j]
+                before = prev_ref[which * rows_ref.shape[0] + firsts[g // 2] + g % 2 * 2 + j]
                 lanes = slice(j * NEIGH_LEN, (j + 1) * NEIGH_LEN)
-                tk[i * 4 + 2 * g + j] = tk[before] + kt[g][:, lanes]
-                tv[i * 4 + 2 * g + j] = tv[before] + vt[g][:, lanes]
+                tk[i * 4 + g % 2 * 2 + j] = tk[before] + kt[g][:, lanes]
+                tv[i * 4 + g % 2 * 2 + j] = tv[before] + vt[g][:, lanes]
 
     def send_out(which, e, n):
         device = source(e, n)
@@ -229,25 +228,31 @@
         def _():
             pltpu.make_async_copy(obuf.at[i], out_ref.at[:, :, cols], out_recv.at[i]).start()
 
+    def send_pair(which, e, m):
+        send_out(which, e, 2 * m)
+        send_out(which, e, 2 * m + 1)
+
     def compute(which, e, begin=0, end=PEERS, held=None):
-        def step(n, carry):
-            i = slot_of(which, e) + n
-            pltpu.make_async_copy(obuf.at[i], rbuf.at[i], in_recv.at[i]).wait()
-            attend(which, e, n)
-
-            @pl.when(n > 0)
+        def step(m, carry):
+            pair = (2 * m, 2 * m + 1)
+            for n in pair:
+                i = slot_of(which, e) + n
+                pltpu.make_async_copy(obuf.at[i], rbuf.at[i], in_recv.at[i]).wait()
+            attend(which, e, pair)
+
+            @pl.when(m > 0)
             def _():
-                send_out(which, e, n - 1)
+                send_pair(which, e, m - 1)
 
             if held is not None:
 
-                @pl.when(n == 0)
+                @pl.when(m == 0)
                 def _():
-                    send_out(held[0], held[1], PEERS - 1)
+                    send_pair(held[0], held[1], PEERS // 2 - 1)
 
             return carry
 
-        lax.fori_loop(begin, end, step, 0)
+        lax.fori_loop(begin // 2, end // 2, step, 0)
 
     def add(refs):
         total = refs[0][...].astype(jnp.float32)
@@ -348,7 +353,7 @@
     compute(NEAR, -2, 6, PEERS)
     scatter_a = scatter_first(NEAR)
     start(scatter_a)
-    send_out(NEAR, -2, PEERS - 1)
+    send_pair(NEAR, -2, PEERS // 2 - 1)
     arrive(scatter_m[2:] + scatter_m2)
     back_first.wait_recv()
 

time: 148 us -> 144 us (0.973); the launches traced: 148 us -> 143 us
  Pallas kernels: 144 us -> 138 us
    pallas_call x1, Pallas kernels: 140 us -> 134 us  [on_device(): pl.pallas_call(kernel, out_shape=(jax.ShapeDtypeStruct((2, TOKENS, querie...]
where the time goes in v5:
time: 144 us; the launch traced here: 143 us
  Pallas kernels  138 us (96%)
  other arithmetic  2.57 us (2%)
    pallas_call x1, Pallas kernels, on_device(): pl.pallas_call(kernel, out_shape=(jax.ShapeDtypeStruct((2, TOKENS, querie...  134 us
    pallas_call x1, Pallas kernels, on_device(): pl.pallas_call(settle, out_shape=(jax.ShapeDtypeStruct(out.shape[1:], bf1...  4.07 us

profile of v5, /device:TPU:1, one launch (start us, length us, event | category | flops | bytes accessed | tf_op | source)
XLA Modules:
  0.0 142.6 jit_solution(17045561700773256180)
XLA Ops:
  0.8 0.8 copy.11
  1.6 0.1 eq.129
  1.7 0.7 select_reduce_fusion.2.rows_ref
  2.5 0.0 copy-start
  2.5 0.1 select_reduce_fusion.1
  2.6 0.1 reduce_max.25
  2.7 0.5 compare_select_fusion.10.last_ref
  3.2 0.1 broadcast_compare_fusion
  3.3 0.4 select_reduce_fusion
  3.7 0.0 copy-done
  3.7 0.6 compare_select_fusion.prev_ref
  4.3 134.2 %retrieval_attention.1 = (bf16[2,128,8192]{2,1,0:T(8,128)(2,1)}, bf16[2,8,128,128]{3,2,1,0:T(8,128)(2,1)}) custom-call(s32[256]{0:T(256)} %copy-done, s32[768]{0:T(1024)} %compare_select_fusion.prev_ref, s32[96]{0:T(128)} %compare_select_fusion.10.last_ref, bf16[128,8192]{1,0:T(8,128)(2,1)} %bitcast.4, bf16[128,8192]{1,0:T(8,128)(2,1)} %bitcast.5, ...), custom_call_target="tpu_custom_call" | custom-call | tf_op jit(solution)/shard_map/retrieval_attention/pallas_call | solution.py:456
  138.5 4.1 %settle.1 = (bf16[128,8192]{1,0:T(8,128)(2,1)}, bf16[128,8192]{1,0:T(8,128)(2,1)}, bf16[8,128,128]{2,1,0:T(8,128)(2,1)}, bf16[8,128,128]{2,1,0:T(8,128)(2,1)}) custom-call(bf16[2,128,8192]{2,1,0:T(8,128)(2,1)} %get-tuple-element.10.out_ref, bf16[2,8,128,128]{3,2,1,0:T(8,128)(2,1)} %get-tuple-element.11.grad_ref), custom_call_target="tpu_custom_call" | custom-call | tf_op jit(solution)/shard_map/settle/pallas_call | solution.py:481
  (5 shorter events, 0.1 us)
Async XLA Ops:
  2.5 1.2 copy-start
